TPU v7x, 32 devices: a whole 2x2x4 slice. The times are simulated.
32 devices in a mesh: row: 8 (over y, x, core), col: 4 (over z).
Axes of the slice: x: 2, y: 2, z: 4, core: 2. Of those that a mesh axis runs over, the one named last changes fastest.
Arguments:
- col_samples: float32 [16, 2, 2048, 128], P('row', None, 'col'), may hold values from -6 to 6
- row_samples: float32 [16, 2, 128, 2048], P('row', None, None, 'col'), may hold values from -6 to 6
- pivot_rows: int32 [16, 128], P('row'), may hold values from 0 to 2047
- rank_blocks: int32 [16], P('row'), may hold values from 1 to 8
- upper_inverse: float32 [2, 2048, 2048], P(None, 'col', 'row'), as said below
- upanel_left: float32 [4, 2, 2048, 128], P('col'), may hold values from -0.125 to 0.125
Outputs:
- panel_right: float32 [16, 2, 128, 2048], P('row', None, None, 'col')
- cores: float32 [16, 4, 2, 128, 128], P('row', 'col')
Inputs may be any that keep to these rules, and one draw needn't show every extreme that they name: `rank_blocks`: the tile's rank is 16 times this. `upper_inverse`: zero below the diagonal in both parts.
All inputs are finite; a program needn't handle non-finite values.
Results may differ from a plain program's by a relative error of at most 0.00007.
Values sent between devices are 32-bit elements; how exact they have to be, the bound alone decides.
A program may use at most 64 MiB of HBM per device.

v0:
```python
import functools
import math

import jax
import jax.numpy as jnp
from jax import lax
from jax.experimental import pallas as pl
from jax.experimental.pallas import tpu as pltpu
from jax.sharding import PartitionSpec as P

RANK_STEP = 16
MESH = pl.DeviceIdType.MESH


def split(x):
    high = x.astype(jnp.bfloat16)
    low = (x - high.astype(jnp.float32)).astype(jnp.bfloat16)
    return high, low


def dot3(xh, xl, uh, ul):
    def single(a, b):
        return jnp.dot(a, b, preferred_element_type=jnp.float32)

    return single(xh, uh) + (single(xh, ul) + single(xl, uh))


def kernel(
    n_rows, n_cols,
    row_ref, u_ref, up_ref, col_ref, piv_ref, rank_ref,
    panel_ref, cores_ref,
    xh, xl, ch, cl, us, ps, pr, fin, lz, lg, ks, kr, eb,
    u_loc, u_send, u_sib, u_fwd, u_recv,
    p_send, p_recv,
    lz_loc, lz_send, lz_recv, lg_loc, lg_send, lg_sib, lg_fwd, lg_recv,
    k_send, k_recv, e_send, e_recv,
):
    r, c = lax.axis_index("row"), lax.axis_index("col")
    chips = n_rows // 2
    nx = math.isqrt(chips)
    ny = chips // nx
    q, h = r // 2, r % 2
    qy, qx = q // nx, q % nx
    tiles, _, ranks, wc = row_ref.shape
    nsub, sw = us.shape[1], us.shape[4]
    wq = lz.shape[1]
    half = tiles * ranks
    sib = (q * 2 + 1 - h, c)

    def ahead(d):
        return ((qy + d // nx) % ny) * nx + (qx + d % nx) % nx

    def behind(d):
        return ((qy + ny - d // nx) % ny) * nx + (qx + nx - d % nx) % nx

    def rcopy(src, dst, ssem, rsem, dev):
        return pltpu.make_async_remote_copy(
            src_ref=src, dst_ref=dst, send_sem=ssem, recv_sem=rsem, device_id=dev, device_id_type=MESH
        )

    def u_out(d, s):
        return rcopy(
            u_ref.at[:, :, s * sw:(s + 1) * sw], us.at[r, s], u_send.at[d, s], u_recv.at[r, s],
            (behind(d) * 2 + h, c),
        )

    def u_side(s):
        return rcopy(u_ref.at[:, :, s * sw:(s + 1) * sw], us.at[r, s], u_sib.at[s], u_recv.at[r, s], sib)

    def u_forward(t, s, b):
        return rcopy(us.at[b, s], us.at[b, s], u_fwd.at[t, s], u_recv.at[b, s], sib)

    def p_up(b, s):
        return rcopy(ps.at[b, s], pr.at[b, s], p_send.at[b, s], p_recv.at[b, s], (r, c + 1))

    def lz_out(k):
        to = (c + k) % n_cols
        start = pl.multiple_of(to * wc + q * wq, wq)
        return rcopy(up_ref.at[0, h, pl.ds(start, wq), :], lz.at[c], lz_send.at[k], lz_recv.at[c], (r, to))

    def lg_out(d):
        return rcopy(lz, lg.at[h, q], lg_send.at[d], lg_recv.at[h, q], (behind(d) * 2 + h, c))

    def lg_side():
        return rcopy(lz, lg.at[h, q], lg_sib.at[0], lg_recv.at[h, q], sib)

    def lg_forward(d):
        b = ahead(d)
        return rcopy(lg.at[h, b], lg.at[h, b], lg_fwd.at[d], lg_recv.at[h, b], sib)

    def k_out(k):
        to = (c + k) % n_cols
        return rcopy(ks.at[k], kr.at[c], k_send.at[k], k_recv.at[c], (r, to))

    def e_out(k):
        return rcopy(eb.at[c], eb.at[c], e_send.at[k], e_recv.at[c], (r, (c + k) % n_cols))

    def each(first, last, body):
        lax.fori_loop(first, last, lambda i, z: (body(i), z)[1], 0)

    own = [
        pltpu.make_async_copy(u_ref.at[:, :, s * sw:(s + 1) * sw], us.at[r, s], u_loc.at[s]) for s in range(nsub)
    ]
    for copy in own:
        copy.start()
    mine = pl.multiple_of(c * wc + q * wq, wq)
    lz_own = pltpu.make_async_copy(up_ref.at[0, h, pl.ds(mine, wq), :], lz.at[c], lz_loc.at[0])
    lz_own.start()
    barrier = pltpu.get_barrier_semaphore()

    def signal(dev):
        pl.semaphore_signal(barrier, inc=1, device_id=dev, device_id_type=MESH)

    signal(sib)
    each(1, chips, lambda d: signal((behind(d) * 2 + h, c)))
    each(1, n_cols, lambda k: signal((r, (c + k) % n_cols)))
    pl.semaphore_wait(barrier, 1 + (chips - 1) + (n_cols - 1))

    @pl.when(q >= c)
    def _():
        for s in range(nsub):
            u_side(s).start()

        @pl.when(q > 0)
        def _():
            for s in range(nsub):
                each(1, chips, lambda d: u_out(d, s).start())

    each(1, n_cols, lambda k: lz_out(k).start())

    for i in range(tiles):
        for p in range(2):
            a, b = split(row_ref[i, p])
            at = pl.ds(p * half + i * ranks, ranks)
            xh[at, :] = a
            xl[at, :] = b

    pos = c * wc + lax.broadcasted_iota(jnp.int32, (wc, ranks), 0)
    parts = []
    for i in range(tiles):
        hit = pos == piv_ref[i:i + 1, :]
        for p in range(2):
            parts.append(jnp.sum(jnp.where(hit, col_ref[i, p], 0.0), axis=0, keepdims=True))
    parts.append(jnp.zeros((eb.shape[1] - 2 * tiles, ranks), jnp.float32))
    eb[c] = jnp.concatenate(parts, axis=0)
    each(1, n_cols, lambda k: e_out(k).start())
    for copy in own:
        copy.wait()

    near = chips * (nsub - 1)
    total = 2 * (near + chips + nsub - 1)
    spread_at = jnp.where(c == 0, 2, 0)
    final_at = jnp.where(c == 0, total - 1, 2 * (near + chips - 1 - c) + 1)

    def finish():
        def pass_on(d2):
            o = ahead(d2)
            rcopy(lz, lg.at[h, o], lg_send.at[d2], lg_recv.at[h, o], sib).wait_recv()
            lg_forward(d2).start()

        each(1, chips, pass_on)

        each(1, n_cols, lambda k: rcopy(
            eb.at[(c + k) % n_cols], eb.at[(c + k) % n_cols], e_send.at[k], e_recv.at[(c + k) % n_cols], sib
        ).wait_recv())
        entries = jnp.sum(eb[...], axis=0)
        lines = []
        levels = lax.broadcasted_iota(jnp.int32, (1, ranks), 1)
        for i in range(tiles):
            er, ei = entries[2 * i:2 * i + 1], entries[2 * i + 1:2 * i + 2]
            keep = (levels < RANK_STEP * rank_ref[i]).astype(jnp.float32)
            mag = jnp.maximum(er * er + ei * ei, 1.0)
            lines.append(keep * er / mag)
            lines.append(-keep * ei / mag)
        lines.append(jnp.zeros((128 - 2 * tiles, ranks), jnp.float32))
        turned = jnp.concatenate(lines, axis=0).T
        for i in range(tiles):
            fr, fi = turned[:, 2 * i:2 * i + 1], turned[:, 2 * i + 1:2 * i + 2]
            lr, li = i * ranks, half + i * ranks
            vr, vi = [], []
            for hh in range(2):
                for s in range(nsub):
                    vr.append(ps[2 * c + hh, s, lr:lr + ranks, :])
                    vi.append(ps[2 * c + hh, s, li:li + ranks, :])
            vr, vi = jnp.concatenate(vr, axis=1), jnp.concatenate(vi, axis=1)
            wr = vr * fr - vi * fi
            wi = vr * fi + vi * fr
            panel_ref[i, 0] = wr
            panel_ref[i, 1] = wi
            a, b = split(wr)
            ch[lr:lr + ranks, :] = a
            cl[lr:lr + ranks, :] = b
            a, b = split(wi)
            ch[li:li + ranks, :] = a
            cl[li:li + ranks, :] = b

        pltpu.make_async_copy(lz, lg.at[h, q], lg_loc.at[0]).wait()
        each(0, chips, lambda o: rcopy(
            lz, lg.at[1 - h, o], lg_sib.at[0], lg_recv.at[1 - h, o], sib
        ).wait_recv())

        def core(k0, carry):
            k = jnp.where(c == 0, n_cols - 1 - k0, (k0 + 1) % n_cols)
            j = (c + k) % n_cols
            lr = lg[0, :, j].reshape(wc, lz.shape[2])
            li = lg[1, :, j].reshape(wc, lz.shape[2])
            rank2 = lz.shape[2]
            uh, ul = split(jnp.concatenate([lr, li], axis=1))
            prod = dot3(ch[...], cl[...], uh, ul)
            real = prod[:half, :rank2] - prod[half:, rank2:]
            imag = prod[:half, rank2:] + prod[half:, :rank2]
            for i in range(tiles):
                ks[k, i, 0] = real[i * ranks:(i + 1) * ranks]
                ks[k, i, 1] = imag[i * ranks:(i + 1) * ranks]

            @pl.when(k > 0)
            def _():
                k_out(k).start()

            return carry

        lax.fori_loop(0, n_cols, core, 0)

    def unit(u, carry):
        slot = u // 2
        t = jnp.where(slot < near, ahead(slot % chips), jnp.maximum(near + chips - 1 - slot, 0))
        s = jnp.where(slot < near, slot // chips, jnp.where(slot < near + chips, nsub - 1, slot - near - chips))
        live = jnp.logical_and(t >= c, jnp.logical_or(slot >= near, t > 0))
        e = u % 2
        b = t * 2 + (h + e) % 2

        @pl.when(u == spread_at)
        def _():
            lz_own.wait()
            each(1, n_cols, lambda k: rcopy(
                lz.at[(c + k) % n_cols], lz.at[(c + k) % n_cols], lz_send.at[k], lz_recv.at[(c + k) % n_cols], sib
            ).wait_recv())
            lg_side().start()
            pltpu.make_async_copy(lz, lg.at[h, q], lg_loc.at[0]).start()
            each(1, chips, lambda d2: lg_out(d2).start())

            @pl.when(jnp.logical_and(q == 0, q >= c))
            def _():
                for s2 in range(nsub):
                    each(1, chips, lambda d2: u_out(d2, s2).start())

        @pl.when(live)
        def _():
            @pl.when(jnp.logical_or(t != q, e > 0))
            def _():
                u_forward(t, s, b).wait_recv()

            @pl.when(jnp.logical_and(t != q, e == 0))
            def _():
                u_forward(t, s, b).start()

            ur, ui = us[b, s, 0], us[b, s, 1]
            uh, ul = split(jnp.concatenate([ur, ui], axis=1))
            prod = dot3(xh[...], xl[...], uh, ul)
            fin[0:half] = prod[:half, :sw] - prod[half:, sw:]
            fin[half:2 * half] = prod[:half, sw:] + prod[half:, :sw]

            @pl.when(c > 0)
            def _():
                rcopy(ps.at[b, s], pr.at[b, s], p_send.at[b, s], p_recv.at[b, s], sib).wait_recv()
                ps[b, s] = fin[...] + pr[b, s]

            @pl.when(c == 0)
            def _():
                ps[b, s] = fin[...]

            @pl.when(t > c)
            def _():
                p_up(b, s).start()

        @pl.when(u == final_at)
        def _():
            finish()

        return carry

    lax.fori_loop(0, total, unit, 0)
    cores_ref[:, 0] = ks[0]

    def gather(k):
        o = (c + k) % n_cols
        rcopy(ks.at[k], kr.at[o], k_send.at[k], k_recv.at[o], sib).wait_recv()
        cores_ref[:, 0] = cores_ref[:, 0] + kr[o]

    each(1, n_cols, gather)

    @pl.when(q >= c)
    def _():
        for s in range(nsub):
            u_side(s).wait_send()

        def left(d):
            for s in range(nsub):
                u_out(d, s).wait_send()

        each(1, chips, left)

    def rest(d):
        t = ahead(d)

        @pl.when(jnp.logical_and(t >= c, d > 0))
        def _():
            for s in range(nsub):
                u_forward(t, s, t * 2 + h).wait_send()

        @pl.when(t > c)
        def _():
            for s in range(nsub):
                for e in range(2):
                    p_up(t * 2 + e, s).wait_send()

        @pl.when(d > 0)
        def _():
            lg_out(d).wait_send()
            lg_forward(d).wait_send()

    each(0, chips, rest)
    lg_side().wait_send()

    def tail(k):
        lz_out(k).wait_send()
        k_out(k).wait_send()
        e_out(k).wait_send()

    each(1, n_cols, tail)


def on_device(n_rows, n_cols, col_samples, row_samples, pivot_rows, rank_blocks, upper_inverse, upanel_left):
    tiles, _, ranks, wc = row_samples.shape
    wr = upper_inverse.shape[2]
    left_ranks = upanel_left.shape[3]
    chips = n_rows // 2
    if chips != n_cols or wc != 2 * wr:
        raise ValueError("unsupported mesh")
    nsub = max(wr // 128, 1)
    sw = wr // nsub
    wq = wc // chips
    m = 2 * tiles * ranks
    f32, bf16 = jnp.float32, jnp.bfloat16
    dma = pltpu.SemaphoreType.DMA
    vmem = pl.BlockSpec(memory_space=pltpu.VMEM)
    hbm = pl.BlockSpec(memory_space=pl.ANY)
    return pl.pallas_call(
        functools.partial(kernel, n_rows, n_cols),
        out_shape=(
            jax.ShapeDtypeStruct((tiles, 2, ranks, wc), f32),
            jax.ShapeDtypeStruct((tiles, 1, 2, ranks, left_ranks), f32),
        ),
        in_specs=[vmem, hbm, hbm, vmem, vmem, pl.BlockSpec(memory_space=pltpu.SMEM)],
        out_specs=(vmem, vmem),
        scratch_shapes=[
            pltpu.VMEM((m, wc), bf16),
            pltpu.VMEM((m, wc), bf16),
            pltpu.VMEM((m, wc), bf16),
            pltpu.VMEM((m, wc), bf16),
            pltpu.VMEM((n_rows, nsub, 2, wc, sw), f32),
            pltpu.VMEM((n_rows, nsub, m, sw), f32),
            pltpu.VMEM((n_rows, nsub, m, sw), f32),
            pltpu.VMEM((m, sw), f32),
            pltpu.VMEM((n_cols, wq, left_ranks), f32),
            pltpu.VMEM((2, chips, n_cols, wq, left_ranks), f32),
            pltpu.VMEM((n_cols, tiles, 2, ranks, left_ranks), f32),
            pltpu.VMEM((n_cols, tiles, 2, ranks, left_ranks), f32),
            pltpu.VMEM((n_cols, -(-2 * tiles // 8) * 8, ranks), f32),
            dma((nsub,)), dma((chips, nsub)), dma((nsub,)), dma((chips, nsub)), dma((n_rows, nsub)),
            dma((n_rows, nsub)), dma((n_rows, nsub)),
            dma((1,)), dma((n_cols,)), dma((n_cols,)), dma((1,)), dma((chips,)), dma((1,)), dma((chips,)),
            dma((2, chips)),
            dma((n_cols,)), dma((n_cols,)), dma((n_cols,)), dma((n_cols,)),
        ],
        compiler_params=pltpu.CompilerParams(
            collective_id=0, has_side_effects=True, vmem_limit_bytes=56 * 1024 * 1024
        ),
    )(row_samples, upper_inverse, upanel_left, col_samples, pivot_rows, rank_blocks)


def solution(mesh):
    in_specs = (
        P("row", None, "col", None),
        P("row", None, None, "col"),
        P("row", None),
        P("row"),
        P(None, "col", "row"),
        P("col", None, None, None),
    )
    out_specs = (P("row", None, None, "col"), P("row", "col", None, None, None))
    body = functools.partial(on_device, mesh.shape["row"], mesh.shape["col"])
    return jax.shard_map(body, mesh=mesh, in_specs=in_specs, out_specs=out_specs, check_vma=False)
```

profile of v0, /device:TPU:25, one launch (start us, length us, event | category | flops | bytes accessed | tf_op | source)
XLA Modules:
  0.0 116.4 jit_solution(13430151088155840327)
XLA Ops:
  0.6 112.7 %shard_map.77 = (f32[2,2,128,512]{3,2,1,0:T(8,128)}, f32[2,1,2,128,128]{4,3,2,1,0:T(8,128)}) custom-call(f32[2,2,128,512]{3,2,1,0:T(8,128)} %row_ref.1, f32[2,512,256]{2,1,0:T(8,128)} %u_ref.1, f32[1,2,2048,128]{3,2,1,0:T(8,128)} %up_ref.1, f32[2,2,512,128]{3,2,1,0:T(8,128)} %col_ref.1, s32[2,128]{1,0:T(2,128)} %piv_ref.1, s32[2]{0:T(128)} %rank_ref.1), custom_call_target="tpu_custom_call" | custom-call | tf_op jit(solution)/shard_map/pallas_call | solution.py:348
  113.4 0.0 copy-start
  113.4 2.3 %copy.10 = f32[2,2,128,512]{3,2,1,0:T(8,128)} copy(f32[2,2,128,512]{3,2,1,0:T(8,128)} %get-tuple-element.4) | data formatting | bytes 2097152
  115.7 0.0 copy-done
  115.7 0.7 copy.11
Async XLA Ops:
  113.4 2.3 %copy-start = (f32[2,1,2,128,128]{4,3,2,1,0:T(8,128)S(1)}, f32[2,1,2,128,128]{4,3,2,1,0:T(8,128)}, u32[]{:S(2)}) copy-start(f32[2,1,2,128,128]{4,3,2,1,0:T(8,128)} %get-tuple-element.5) | copy-start | bytes 786436
where the time goes:
time: 117 us; the launch traced here: 116 us
  Pallas kernels  113 us (97%)
  local copies, waits for them, and re-layouts  3.01 us (3%)
    pallas_call x1, Pallas kernels, on_device(): pl.pallas_call(functools.partial(kernel, n_rows, n_cols), out_shape=(jax....  113 us
    unnamed x4, local copies, waits for them, and re-layouts  3.01 us

commit v1 on v0

--- a/solution.py
+++ b/solution.py
@@ -330,6 +330,573 @@
     each(1, n_cols, tail)
 
 
+def paired_kernel(
+    n_rows, n_cols,
+    row_ref, u_ref, up_ref, col_ref, piv_ref, rank_ref,
+    panel_ref, cores_ref,
+    xh, xl, x0, ch, cl, us, ps, pr, lz, lg, ks, ku, kd, eb,
+    u_loc, nat_x, nat_y, nat_fwd, full1, half1,
+    lift, full0, half0, lift_x, lift_y, lift_fx, lift_fy,
+    side_send, side_recv, x_send, x_recv, p_send, p_recv,
+    lz_loc, lz_send, lz_recv, lg_loc, lg_send, lg_sib, lg_fwd, lg_recv,
+    ku_send, ku_recv, kd_send, kd_recv, e_send, e_recv,
+):
+    r, c = lax.axis_index("row"), lax.axis_index("col")
+    chips = n_rows // 2
+    nx = math.isqrt(chips)
+    q, h = r // 2, r % 2
+    qy, qx = q // nx, q % nx
+    xn, yn, dn = qy * nx + 1 - qx, (1 - qy) * nx + qx, (1 - qy) * nx + 1 - qx
+    tiles, _, ranks, wc = row_ref.shape
+    nsub, sw = us.shape[1], us.shape[5]
+    wq = lz.shape[1]
+    sib = (q * 2 + 1 - h, c)
+    to_x, to_y = (xn * 2 + h, c), (yn * 2 + h, c)
+    stages = nsub * (n_cols - 1)
+    early = nsub * (n_cols - 2)
+
+    def ahead(d):
+        return ((qy + d // nx) % nx) * nx + (qx + d % nx) % nx
+
+    def rcopy(src, dst, ssem, rsem, dev):
+        return pltpu.make_async_remote_copy(
+            src_ref=src, dst_ref=dst, send_sem=ssem, recv_sem=rsem, device_id=dev, device_id_type=MESH
+        )
+
+    def each(first, last, body):
+        lax.fori_loop(first, last, lambda i, z: (body(i), z)[1], 0)
+
+    def ts(i):
+        return jnp.where(c == 0, 0, n_cols - 1 - i // nsub), i % nsub
+
+    def active(i):
+        t, _ = ts(i)
+        return jnp.logical_and(i < stages, jnp.where(c == 0, i < nsub, t >= c))
+
+    def ucols(s):
+        return u_ref.at[:, :, pl.ds(pl.multiple_of(s * sw, sw), sw)]
+
+    def local_u(s):
+        return pltpu.make_async_copy(ucols(s), us.at[r, s, 1], u_loc.at[s])
+
+    def nat_out(s, dev, sem):
+        return rcopy(ucols(s), us.at[r, s, 1], sem.at[s], full1.at[q, s], dev)
+
+    def nat_full(t, s):
+        b = 2 * t + h
+        return rcopy(us.at[b, s, 1], us.at[b, s, 1], nat_fwd.at[t, s], full1.at[t, s], sib)
+
+    def nat_half(t, s, k, dev):
+        b = 2 * t + h
+        part = us.at[b, s, 1, :, k * (wc // 2):(k + 1) * (wc // 2), :]
+        return rcopy(part, part, nat_fwd.at[t, s], half1.at[t, s, k], dev)
+
+    def piece(b, s, g):
+        return us.at[b, s, 0, :, pl.ds(pl.multiple_of(g * wq, wq), wq), :]
+
+    def lift_out(s, g):
+        rows = pl.ds(pl.multiple_of(g * wq, wq), wq)
+        src = u_ref.at[:, rows, pl.ds(pl.multiple_of(s * sw, sw), sw)]
+        return rcopy(src, piece(r, s, g), lift.at[s, g], full0.at[q, s, g], (g * 2 + h, 1))
+
+    def lift_full(t, s, g, sem, dev):
+        p = piece(2 * t + h, s, g)
+        return rcopy(p, p, sem.at[t, s], full0.at[t, s, g], dev)
+
+    def lift_half(t, s, g, k, sem, dev):
+        rows = pl.ds(pl.multiple_of(g * wq + k * (wq // 2), wq // 2), wq // 2)
+        p = us.at[2 * t + h, s, 0, :, rows, :]
+        return rcopy(p, p, sem.at[t, s], half0.at[t, s, k], dev)
+
+    def side(t, s, kk, b):
+        return rcopy(us.at[b, s, kk], us.at[b, s, kk], side_send.at[t, s, kk], side_recv.at[t, s, kk], sib)
+
+    def x_up(m):
+        return rcopy(row_ref.at[m], x0.at[m], x_send.at[m], x_recv.at[m], (r, c + 1))
+
+    def p_up(b, s, m):
+        return rcopy(ps.at[b, s, m], pr.at[b, s, m], p_send.at[b, s, m], p_recv.at[b, s, m], (r, c + 1))
+
+    def lz_out(k):
+        to = (c + k) % n_cols
+        start = pl.multiple_of(to * wc + q * wq, wq)
+        return rcopy(up_ref.at[0, h, pl.ds(start, wq), :], lz.at[c], lz_send.at[k], lz_recv.at[c], (r, to))
+
+    def lg_out(d):
+        return rcopy(lz, lg.at[h, q], lg_send.at[d], lg_recv.at[h, q], (ahead(d) * 2 + h, c))
+
+    def lg_side():
+        return rcopy(lz, lg.at[h, q], lg_sib.at[0], lg_recv.at[h, q], sib)
+
+    def lg_forward(d):
+        b = ahead(d)
+        return rcopy(lg.at[h, b], lg.at[h, b], lg_fwd.at[d], lg_recv.at[h, b], sib)
+
+    def k_up(j, m):
+        return rcopy(ks.at[j, m], ku.at[j, m], ku_send.at[j, m], ku_recv.at[j, m], (r, c + 1))
+
+    def k_down(j, m):
+        return rcopy(ks.at[j, m], kd.at[c, m], kd_send.at[j, m], kd_recv.at[c, m], (r, j))
+
+    def e_out(k):
+        return rcopy(eb.at[c], eb.at[c], e_send.at[k], e_recv.at[c], (r, (c + k) % n_cols))
+
+    mine = pl.multiple_of(c * wc + q * wq, wq)
+    lz_own = pltpu.make_async_copy(up_ref.at[0, h, pl.ds(mine, wq), :], lz.at[c], lz_loc.at[0])
+    lz_own.start()
+    barrier = pltpu.get_barrier_semaphore()
+
+    def signal(dev):
+        pl.semaphore_signal(barrier, inc=1, device_id=dev, device_id_type=MESH)
+
+    signal(sib)
+    each(1, chips, lambda d: signal((ahead(d) * 2 + h, c)))
+    each(1, n_cols, lambda k: signal((r, (c + k) % n_cols)))
+
+    @pl.when(c < 2)
+    def _():
+        each(1, chips, lambda d: signal((ahead(d) * 2 + h, 1 - c)))
+
+    pl.semaphore_wait(barrier, 1 + (chips - 1) + (n_cols - 1) + jnp.where(c < 2, chips - 1, 0))
+
+    def native_out(i):
+        t, s = ts(i)
+
+        @pl.when(jnp.logical_and(active(i), q == t))
+        def _():
+            nat_out(s, to_x, nat_x).start()
+            nat_out(s, to_y, nat_y).start()
+            local_u(s).start()
+
+    def lift_in(i):
+        t, s = ts(i)
+
+        @pl.when(jnp.logical_and(active(i), c == 1))
+        def _():
+            lift_full(t, s, q, lift_x, sib).wait_recv()
+            lift_full(t, s, q, lift_x, to_x).start()
+            lift_full(t, s, q, lift_y, to_y).start()
+
+    def relay(i):
+        t, s = ts(i)
+
+        @pl.when(active(i))
+        def _():
+            @pl.when(xn == t)
+            def _():
+                nat_full(t, s).wait_recv()
+                nat_half(t, s, 0, to_y).start()
+
+            @pl.when(yn == t)
+            def _():
+                nat_full(t, s).wait_recv()
+                nat_half(t, s, 1, to_x).start()
+
+            @pl.when(c == 1)
+            def _():
+                lift_full(t, s, xn, lift_x, sib).wait_recv()
+                lift_half(t, s, xn, 0, lift_fy, to_y).start()
+                lift_full(t, s, yn, lift_x, sib).wait_recv()
+                lift_half(t, s, yn, 1, lift_fx, to_x).start()
+
+    def collect(i):
+        t, s = ts(i)
+
+        @pl.when(active(i))
+        def _():
+            @pl.when(dn == t)
+            def _():
+                nat_half(t, s, 0, sib).wait_recv()
+                nat_half(t, s, 1, sib).wait_recv()
+
+            @pl.when(q == t)
+            def _():
+                local_u(s).wait()
+
+            side(t, s, 1, 2 * t + h).start()
+
+            @pl.when(c == 1)
+            def _():
+                lift_half(t, s, dn, 0, lift_fy, sib).wait_recv()
+                lift_half(t, s, dn, 1, lift_fx, sib).wait_recv()
+                side(t, s, 0, 2 * t + h).start()
+
+    def pump(i):
+        @pl.when(i >= early)
+        def _():
+            lift_in(i)
+
+        relay(i)
+        native_out(i + 2)
+
+        @pl.when(i + 1 < early)
+        def _():
+            lift_in(i + 1)
+
+        collect(i)
+
+    def lifts():
+        for s in range(nsub):
+            each(0, chips, lambda g: lift_out(s, g).start())
+
+    @pl.when(jnp.logical_and(c == 0, q == chips - 1))
+    def _():
+        lifts()
+
+    @pl.when(c == 0)
+    def _():
+        x_up(0).start()
+
+    native_out(0)
+    native_out(1)
+    each(1, n_cols, lambda k: lz_out(k).start())
+
+    @pl.when(c == 0)
+    def _():
+        for m in range(1, tiles):
+            x_up(m).start()
+
+    for m in range(tiles):
+        for p in range(2):
+            a, b = split(row_ref[m, p])
+            xh[1, m, p * ranks:(p + 1) * ranks, :] = a
+            xl[1, m, p * ranks:(p + 1) * ranks, :] = b
+
+    pos = c * wc + lax.broadcasted_iota(jnp.int32, (wc, ranks), 0)
+    parts = []
+    for i in range(tiles):
+        hit = pos == piv_ref[i:i + 1, :]
+        for p in range(2):
+            parts.append(jnp.sum(jnp.where(hit, col_ref[i, p], 0.0), axis=0, keepdims=True))
+    parts.append(jnp.zeros((eb.shape[1] - 2 * tiles, ranks), jnp.float32))
+    eb[c] = jnp.concatenate(parts, axis=0)
+    each(1, n_cols, lambda k: e_out(k).start())
+
+    def spread():
+        lz_own.wait()
+        each(1, n_cols, lambda k: rcopy(
+            lz.at[(c + k) % n_cols], lz.at[(c + k) % n_cols], lz_send.at[k], lz_recv.at[(c + k) % n_cols], sib
+        ).wait_recv())
+        lg_side().start()
+        pltpu.make_async_copy(lz, lg.at[h, q], lg_loc.at[0]).start()
+        each(1, chips, lambda d: lg_out(d).start())
+
+    lift_in(0)
+
+    @pl.when(c == 1)
+    def _():
+        pump(0)
+
+    @pl.when(c != 1)
+    def _():
+        each(0, early, pump)
+
+    @pl.when(c == 0)
+    def _():
+        for m in range(tiles):
+            x_up(m).wait_send()
+
+            @pl.when(q == chips - 2 - m)
+            def _():
+                lifts()
+
+        @pl.when(jnp.logical_and(q > 0, q < chips - 1 - tiles))
+        def _():
+            lifts()
+
+    @pl.when(c != 1)
+    def _():
+        spread()
+
+    def gather():
+        def pass_on(d):
+            o = ahead(d)
+            rcopy(lz, lg.at[h, o], lg_send.at[d], lg_recv.at[h, o], sib).wait_recv()
+            lg_forward(d).start()
+
+        each(1, chips, pass_on)
+        each(1, n_cols, lambda k: rcopy(
+            eb.at[(c + k) % n_cols], eb.at[(c + k) % n_cols], e_send.at[k], e_recv.at[(c + k) % n_cols], sib
+        ).wait_recv())
+        pltpu.make_async_copy(lz, lg.at[h, q], lg_loc.at[0]).wait()
+        each(0, chips, lambda o: rcopy(
+            lz, lg.at[1 - h, o], lg_sib.at[0], lg_recv.at[1 - h, o], sib
+        ).wait_recv())
+
+    def finish(m):
+        @pl.when(m == 0)
+        def _():
+            gather()
+
+        entries = jnp.sum(eb[...], axis=0)
+        lines = []
+        levels = lax.broadcasted_iota(jnp.int32, (1, ranks), 1)
+        for i in range(tiles):
+            er, ei = entries[2 * i:2 * i + 1], entries[2 * i + 1:2 * i + 2]
+            keep = (levels < RANK_STEP * rank_ref[i]).astype(jnp.float32)
+            mag = jnp.maximum(er * er + ei * ei, 1.0)
+            lines.append(keep * er / mag)
+            lines.append(-keep * ei / mag)
+        factor_r, factor_i = lines[0], lines[1]
+        for i in range(1, tiles):
+            factor_r = jnp.where(m == i, lines[2 * i], factor_r)
+            factor_i = jnp.where(m == i, lines[2 * i + 1], factor_i)
+        pad = jnp.zeros((126, ranks), jnp.float32)
+        turned = jnp.concatenate([factor_r, factor_i, pad], axis=0).T
+        fr, fi = turned[:, 0:1], turned[:, 1:2]
+        vr, vi = [], []
+        for hh in range(2):
+            for s in range(nsub):
+                vr.append(ps[2 * c + hh, s, m, 0])
+                vi.append(ps[2 * c + hh, s, m, 1])
+        vr, vi = jnp.concatenate(vr, axis=1), jnp.concatenate(vi, axis=1)
+        wr = vr * fr - vi * fi
+        wi = vr * fi + vi * fr
+        panel_ref[m, 0] = wr
+        panel_ref[m, 1] = wi
+        a, b = split(wr)
+        ch[0:ranks, :] = a
+        cl[0:ranks, :] = b
+        a, b = split(wi)
+        ch[ranks:2 * ranks, :] = a
+        cl[ranks:2 * ranks, :] = b
+
+        def core(j, carry):
+            rank2 = lz.shape[2]
+            lr = lg[0, :, j].reshape(wc, rank2)
+            li = lg[1, :, j].reshape(wc, rank2)
+            uh, ul = split(jnp.concatenate([lr, li], axis=1))
+            prod = dot3(ch[...], cl[...], uh, ul)
+            ks[j, m, 0] = prod[:ranks, :rank2] - prod[ranks:, rank2:]
+            ks[j, m, 1] = prod[:ranks, rank2:] + prod[ranks:, :rank2]
+
+            @pl.when(j < c)
+            def _():
+                k_down(j, m).start()
+
+            @pl.when(jnp.logical_and(c == 0, j > 0))
+            def _():
+                k_up(j, m).start()
+
+            return carry
+
+        lax.fori_loop(0, n_cols, core, 0)
+
+    head = early * tiles
+    tail = stages - early
+    total = head + tail * tiles
+    first_final = jnp.where(c == 0, nsub, (n_cols - c) * nsub)
+    final0 = jnp.where(c == 1, head + tail - 1, first_final - 1)
+    final1 = jnp.where(c == 1, tail, early)
+
+    def unit(u, carry):
+        i = jnp.where(u < head, u % early, early + (u - head) % tail)
+        m = jnp.where(u < head, u // early, (u - head) // tail)
+        t, s = ts(i)
+
+        @pl.when(active(i))
+        def _():
+            @pl.when(jnp.logical_and(c == 1, jnp.logical_and(u < head, u % early == 0)))
+            def _():
+                x_up(m).wait_recv()
+                for p in range(2):
+                    a, b = split(x0[m, p])
+                    xh[0, m, p * ranks:(p + 1) * ranks, :] = a
+                    xl[0, m, p * ranks:(p + 1) * ranks, :] = b
+
+            for e in range(2):
+                b = 2 * t + (h + e) % 2
+
+                if e == 1:
+                    @pl.when(m == 0)
+                    def _():
+                        side(t, s, 1, b).wait_recv()
+
+                        @pl.when(c == 1)
+                        def _():
+                            side(t, s, 0, b).wait_recv()
+
+                def product(kk):
+                    uh, ul = split(jnp.concatenate([us[b, s, kk, 0], us[b, s, kk, 1]], axis=1))
+                    prod = dot3(xh[kk, m], xl[kk, m], uh, ul)
+                    real = prod[:ranks, :sw] - prod[ranks:, sw:]
+                    imag = prod[:ranks, sw:] + prod[ranks:, :sw]
+                    return real, imag
+
+                real, imag = product(1)
+
+                @pl.when(c == 1)
+                def _():
+                    real0, imag0 = product(0)
+                    ps[b, s, m, 0] = real + real0
+                    ps[b, s, m, 1] = imag + imag0
+
+                @pl.when(c == 0)
+                def _():
+                    ps[b, s, m, 0] = real
+                    ps[b, s, m, 1] = imag
+
+                @pl.when(c > 1)
+                def _():
+                    p_up(b, s, m).wait_recv()
+                    ps[b, s, m, 0] = real + pr[b, s, m, 0]
+                    ps[b, s, m, 1] = imag + pr[b, s, m, 1]
+
+                @pl.when(t > c)
+                def _():
+                    p_up(b, s, m).start()
+
+        @pl.when(jnp.logical_or(u == final0, u == final0 + final1))
+        def _():
+            finish(m)
+
+        @pl.when(c == 1)
+        def _():
+            @pl.when(u + 1 < early)
+            def _():
+                pump(u + 1)
+
+            @pl.when(u == early - 1)
+            def _():
+                spread()
+
+            @pl.when(jnp.logical_and(u >= early + 1, u < early + 1 + tail))
+            def _():
+                pump(u - 1)
+
+        return carry
+
+    lax.fori_loop(0, total, unit, 0)
+
+    @pl.when(c > 0)
+    def _():
+        for m in range(tiles):
+            def lower(j):
+                k_up(j, m).wait_recv()
+                ks[j, m] = ks[j, m] + ku[j, m]
+
+                @pl.when(j > c)
+                def _():
+                    k_up(j, m).start()
+
+            each(c, n_cols, lower)
+
+    for m in range(tiles):
+        cores_ref[m, 0] = ks[c, m]
+
+        def upper(o):
+            rcopy(ks.at[c, m], kd.at[o, m], kd_send.at[c, m], kd_recv.at[o, m], sib).wait_recv()
+            cores_ref[m, 0] = cores_ref[m, 0] + kd[o, m]
+
+        each(c + 1, n_cols, upper)
+
+    @pl.when(jnp.logical_and(c == 0, q > 0))
+    def _():
+        for s in range(nsub):
+            each(0, chips, lambda g: lift_out(s, g).wait_send())
+
+    def drain(i):
+        t, s = ts(i)
+
+        @pl.when(active(i))
+        def _():
+            @pl.when(q == t)
+            def _():
+                nat_out(s, to_x, nat_x).wait_send()
+                nat_out(s, to_y, nat_y).wait_send()
+
+            @pl.when(jnp.logical_or(xn == t, yn == t))
+            def _():
+                nat_half(t, s, 0, sib).wait_send()
+
+            side(t, s, 1, 2 * t + h).wait_send()
+
+            @pl.when(c == 1)
+            def _():
+                lift_full(t, s, q, lift_x, sib).wait_send()
+                lift_full(t, s, q, lift_y, sib).wait_send()
+                lift_half(t, s, xn, 0, lift_fy, sib).wait_send()
+                lift_half(t, s, yn, 1, lift_fx, sib).wait_send()
+                side(t, s, 0, 2 * t + h).wait_send()
+
+            @pl.when(t > c)
+            def _():
+                for m in range(tiles):
+                    for e in range(2):
+                        p_up(2 * t + e, s, m).wait_send()
+
+    each(0, stages, drain)
+
+    def tail_l(d):
+        lg_out(d).wait_send()
+        lg_forward(d).wait_send()
+
+    each(1, chips, tail_l)
+    lg_side().wait_send()
+
+    def tail_z(k):
+        lz_out(k).wait_send()
+        e_out(k).wait_send()
+
+    each(1, n_cols, tail_z)
+    for m in range(tiles):
+        each(0, c, lambda j: k_down(j, m).wait_send())
+        each(c + 1, n_cols, lambda j: k_up(j, m).wait_send())
+
+
+def paired(n_rows, n_cols, col_samples, row_samples, pivot_rows, rank_blocks, upper_inverse, upanel_left):
+    tiles, _, ranks, wc = row_samples.shape
+    wr = upper_inverse.shape[2]
+    left_ranks = upanel_left.shape[3]
+    chips = n_rows // 2
+    nsub = wr // 128
+    sw = wr // nsub
+    wq = wc // chips
+    f32, bf16 = jnp.float32, jnp.bfloat16
+    dma = pltpu.SemaphoreType.DMA
+    vmem = pl.BlockSpec(memory_space=pltpu.VMEM)
+    hbm = pl.BlockSpec(memory_space=pl.ANY)
+    sums = pltpu.VMEM((n_rows, nsub, tiles, 2, ranks, sw), f32)
+    return pl.pallas_call(
+        functools.partial(paired_kernel, n_rows, n_cols),
+        out_shape=(
+            jax.ShapeDtypeStruct((tiles, 2, ranks, wc), f32),
+            jax.ShapeDtypeStruct((tiles, 1, 2, ranks, left_ranks), f32),
+        ),
+        in_specs=[vmem, hbm, hbm, vmem, vmem, pl.BlockSpec(memory_space=pltpu.SMEM)],
+        out_specs=(vmem, vmem),
+        scratch_shapes=[
+            pltpu.VMEM((2, tiles, 2 * ranks, wc), bf16),
+            pltpu.VMEM((2, tiles, 2 * ranks, wc), bf16),
+            pltpu.VMEM((tiles, 2, ranks, wc), f32),
+            pltpu.VMEM((2 * ranks, wc), bf16),
+            pltpu.VMEM((2 * ranks, wc), bf16),
+            pltpu.VMEM((n_rows, nsub, 2, 2, wc, sw), f32),
+            sums,
+            sums,
+            pltpu.VMEM((n_cols, wq, left_ranks), f32),
+            pltpu.VMEM((2, chips, n_cols, wq, left_ranks), f32),
+            pltpu.VMEM((n_cols, tiles, 2, ranks, left_ranks), f32),
+            pltpu.VMEM((n_cols, tiles, 2, ranks, left_ranks), f32),
+            pltpu.VMEM((n_cols, tiles, 2, ranks, left_ranks), f32),
+            pltpu.VMEM((n_cols, -(-2 * tiles // 8) * 8, ranks), f32),
+            dma((nsub,)), dma((nsub,)), dma((nsub,)), dma((n_cols, nsub)), dma((n_cols, nsub)),
+            dma((n_cols, nsub, 2)),
+            dma((nsub, chips)), dma((n_cols, nsub, chips)), dma((n_cols, nsub, 2)),
+            dma((n_cols, nsub)), dma((n_cols, nsub)), dma((n_cols, nsub)), dma((n_cols, nsub)),
+            dma((n_cols, nsub, 2)), dma((n_cols, nsub, 2)), dma((tiles,)), dma((tiles,)),
+            dma((n_rows, nsub, tiles)), dma((n_rows, nsub, tiles)),
+            dma((1,)), dma((n_cols,)), dma((n_cols,)), dma((1,)), dma((chips,)), dma((1,)), dma((chips,)),
+            dma((2, chips)),
+            dma((n_cols, tiles)), dma((n_cols, tiles)), dma((n_cols, tiles)), dma((n_cols, tiles)),
+            dma((n_cols,)), dma((n_cols,)),
+        ],
+        compiler_params=pltpu.CompilerParams(
+            collective_id=0, has_side_effects=True, vmem_limit_bytes=56 * 1024 * 1024
+        ),
+    )(row_samples, upper_inverse, upanel_left, col_samples, pivot_rows, rank_blocks)
+
+
 def on_device(n_rows, n_cols, col_samples, row_samples, pivot_rows, rank_blocks, upper_inverse, upanel_left):
     tiles, _, ranks, wc = row_samples.shape
     wr = upper_inverse.shape[2]
@@ -337,6 +904,10 @@
     chips = n_rows // 2
     if chips != n_cols or wc != 2 * wr:
         raise ValueError("unsupported mesh")
+    if chips == 4 and wr % 128 == 0:
+        return paired(
+            n_rows, n_cols, col_samples, row_samples, pivot_rows, rank_blocks, upper_inverse, upanel_left
+        )
     nsub = max(wr // 128, 1)
     sw = wr // nsub
     wq = wc // chips

time: 117 us -> 172 us (1.47)
  the two profiles are of different devices: /device:TPU:25 before, /device:TPU:28 now
where the time goes in v1:
time: 172 us; the launch traced here: 171 us
  Pallas kernels  168 us (98%)
  local copies, waits for them, and re-layouts  3.01 us (2%)
    pallas_call x1, Pallas kernels, paired(): pl.pallas_call(functools.partial(paired_kernel, n_rows, n_cols), out_shap...  168 us

profile of v1, /device:TPU:28, one launch (start us, length us, event | category | flops | bytes accessed | tf_op | source)
XLA Modules:
  0.0 171.3 jit_solution(5234405319006999979)
XLA Ops:
  0.6 167.7 %shard_map.77 = (f32[2,2,128,512]{3,2,1,0:T(8,128)}, f32[2,1,2,128,128]{4,3,2,1,0:T(8,128)}) custom-call(f32[2,2,128,512]{3,2,1,0:T(8,128)} %row_ref.1, f32[2,512,256]{2,1,0:T(8,128)} %u_ref.1, f32[1,2,2048,128]{3,2,1,0:T(8,128)} %up_ref.1, f32[2,2,512,128]{3,2,1,0:T(8,128)} %col_ref.1, s32[2,128]{1,0:T(2,128)} %piv_ref.1, s32[2]{0:T(128)} %rank_ref.1), custom_call_target="tpu_custom_call" | custom-call | tf_op jit(solution)/shard_map/pallas_call | solution.py:860
  168.3 0.0 copy-start
  168.3 2.3 %copy.10 = f32[2,2,128,512]{3,2,1,0:T(8,128)} copy(f32[2,2,128,512]{3,2,1,0:T(8,128)} %get-tuple-element.4) | data formatting | bytes 2097152
  170.6 0.0 copy-done
  170.6 0.7 copy.11
Async XLA Ops:
  168.3 2.3 %copy-start = (f32[2,1,2,128,128]{4,3,2,1,0:T(8,128)S(1)}, f32[2,1,2,128,128]{4,3,2,1,0:T(8,128)}, u32[]{:S(2)}) copy-start(f32[2,1,2,128,128]{4,3,2,1,0:T(8,128)} %get-tuple-element.5) | copy-start | bytes 786436

commit v2 on v1

--- a/solution.py
+++ b/solution.py
@@ -334,12 +334,12 @@
     n_rows, n_cols,
     row_ref, u_ref, up_ref, col_ref, piv_ref, rank_ref,
     panel_ref, cores_ref,
-    xh, xl, x0, ch, cl, us, ps, pr, lz, lg, ks, ku, kd, eb,
-    u_loc, nat_x, nat_y, nat_fwd, full1, half1,
+    xh, xl, x0, ch, cl, us, ps, pr, pq, pin, lg, ks, kd, eb,
+    u_loc, nat_x, nat_y, nat_fwd, full1, near1, half1,
     lift, full0, half0, lift_x, lift_y, lift_fx, lift_fy,
-    side_send, side_recv, x_send, x_recv, p_send, p_recv,
-    lz_loc, lz_send, lz_recv, lg_loc, lg_send, lg_sib, lg_fwd, lg_recv,
-    ku_send, ku_recv, kd_send, kd_recv, e_send, e_recv,
+    side_send, side_recv, x_send, x_recv, p_send, p_recv, q_send, q_recv,
+    l_loc, l_send, l_recv, g_send, g_recv, l_side, l_got,
+    k_send, k_recv, e_send, e_recv,
 ):
     r, c = lax.axis_index("row"), lax.axis_index("col")
     chips = n_rows // 2
@@ -349,11 +349,12 @@
     xn, yn, dn = qy * nx + 1 - qx, (1 - qy) * nx + qx, (1 - qy) * nx + 1 - qx
     tiles, _, ranks, wc = row_ref.shape
     nsub, sw = us.shape[1], us.shape[5]
-    wq = lz.shape[1]
+    wq = wc // chips
+    rank2 = lg.shape[4]
+    width = n_cols - 2
     sib = (q * 2 + 1 - h, c)
     to_x, to_y = (xn * 2 + h, c), (yn * 2 + h, c)
-    stages = nsub * (n_cols - 1)
-    early = nsub * (n_cols - 2)
+    stages = 2 * nsub
 
     def ahead(d):
         return ((qy + d // nx) % nx) * nx + (qx + d % nx) % nx
@@ -367,11 +368,14 @@
         lax.fori_loop(first, last, lambda i, z: (body(i), z)[1], 0)
 
     def ts(i):
-        return jnp.where(c == 0, 0, n_cols - 1 - i // nsub), i % nsub
+        t = jnp.where(c == 0, 1 - i // nsub, n_cols - 1 - i % width)
+        return t, jnp.where(c == 0, i % nsub, i // width)
 
     def active(i):
-        t, _ = ts(i)
-        return jnp.logical_and(i < stages, jnp.where(c == 0, i < nsub, t >= c))
+        return ts(i)[0] >= c
+
+    def lifted(i):
+        return jnp.logical_and(c < 2, ts(i)[0] > 0)
 
     def ucols(s):
         return u_ref.at[:, :, pl.ds(pl.multiple_of(s * sw, sw), sw)]
@@ -379,17 +383,21 @@
     def local_u(s):
         return pltpu.make_async_copy(ucols(s), us.at[r, s, 1], u_loc.at[s])
 
-    def nat_out(s, dev, sem):
-        return rcopy(ucols(s), us.at[r, s, 1], sem.at[s], full1.at[q, s], dev)
+    def nat_out(s):
+        return rcopy(ucols(s), us.at[r, s, 1], nat_x.at[s], full1.at[q, s], to_x)
+
+    def nat_near(s, k):
+        rows = slice(k * (wc // 2), (k + 1) * (wc // 2))
+        src = u_ref.at[:, rows, pl.ds(pl.multiple_of(s * sw, sw), sw)]
+        return rcopy(src, us.at[r, s, 1, :, rows, :], nat_y.at[s, k], near1.at[q, s, k], to_y)
 
     def nat_full(t, s):
         b = 2 * t + h
-        return rcopy(us.at[b, s, 1], us.at[b, s, 1], nat_fwd.at[t, s], full1.at[t, s], sib)
-
-    def nat_half(t, s, k, dev):
-        b = 2 * t + h
-        part = us.at[b, s, 1, :, k * (wc // 2):(k + 1) * (wc // 2), :]
-        return rcopy(part, part, nat_fwd.at[t, s], half1.at[t, s, k], dev)
+        return rcopy(us.at[b, s, 1], us.at[b, s, 1], nat_fwd.at[t, s, 0], full1.at[t, s], sib)
+
+    def nat_half(t, s, k, got):
+        part = us.at[2 * t + h, s, 1, :, k * (wc // 2):(k + 1) * (wc // 2), :]
+        return rcopy(part, part, nat_fwd.at[t, s, k], got.at[t, s, k], to_x)
 
     def piece(b, s, g):
         return us.at[b, s, 0, :, pl.ds(pl.multiple_of(g * wq, wq), wq), :]
@@ -397,7 +405,7 @@
     def lift_out(s, g):
         rows = pl.ds(pl.multiple_of(g * wq, wq), wq)
         src = u_ref.at[:, rows, pl.ds(pl.multiple_of(s * sw, sw), sw)]
-        return rcopy(src, piece(r, s, g), lift.at[s, g], full0.at[q, s, g], (g * 2 + h, 1))
+        return rcopy(src, piece(r, s, g), lift.at[s, g], full0.at[q, s, g], (g * 2 + h, 1 - c))
 
     def lift_full(t, s, g, sem, dev):
         p = piece(2 * t + h, s, g)
@@ -411,39 +419,52 @@
     def side(t, s, kk, b):
         return rcopy(us.at[b, s, kk], us.at[b, s, kk], side_send.at[t, s, kk], side_recv.at[t, s, kk], sib)
 
-    def x_up(m):
-        return rcopy(row_ref.at[m], x0.at[m], x_send.at[m], x_recv.at[m], (r, c + 1))
+    def x_swap(m):
+        return rcopy(row_ref.at[m], x0.at[m], x_send.at[m], x_recv.at[m], (r, 1 - c))
 
     def p_up(b, s, m):
         return rcopy(ps.at[b, s, m], pr.at[b, s, m], p_send.at[b, s, m], p_recv.at[b, s, m], (r, c + 1))
 
-    def lz_out(k):
-        to = (c + k) % n_cols
-        start = pl.multiple_of(to * wc + q * wq, wq)
-        return rcopy(up_ref.at[0, h, pl.ds(start, wq), :], lz.at[c], lz_send.at[k], lz_recv.at[c], (r, to))
-
-    def lg_out(d):
-        return rcopy(lz, lg.at[h, q], lg_send.at[d], lg_recv.at[h, q], (ahead(d) * 2 + h, c))
-
-    def lg_side():
-        return rcopy(lz, lg.at[h, q], lg_sib.at[0], lg_recv.at[h, q], sib)
-
-    def lg_forward(d):
-        b = ahead(d)
-        return rcopy(lg.at[h, b], lg.at[h, b], lg_fwd.at[d], lg_recv.at[h, b], sib)
-
-    def k_up(j, m):
-        return rcopy(ks.at[j, m], ku.at[j, m], ku_send.at[j, m], ku_recv.at[j, m], (r, c + 1))
-
-    def k_down(j, m):
-        return rcopy(ks.at[j, m], kd.at[c, m], kd_send.at[j, m], kd_recv.at[c, m], (r, j))
+    def l_part(j, nb, g):
+        return lg.at[h, nb, j, pl.ds(pl.multiple_of(g * wq, wq), wq), :]
+
+    def l_out(o, nb):
+        rows = pl.ds(pl.multiple_of((o + nb) * wc + q * wq, wq), wq)
+        return rcopy(up_ref.at[0, h, rows, :], l_part(c, nb, q), l_send.at[o, nb], l_recv.at[c, nb], (r, o))
+
+    def g_out(j, nb, d):
+        p = l_part(j, nb, q)
+        return rcopy(p, p, g_send.at[j, nb, d], g_recv.at[j, nb, q], (ahead(d) * 2 + h, c))
+
+    def l_sib(j, nb, comp):
+        return rcopy(lg.at[comp, nb, j], lg.at[comp, nb, j], l_side.at[j, nb], l_got.at[j, nb], sib)
+
+    def l_own(nb):
+        rows = pl.ds(pl.multiple_of((c + nb) * wc, wc), wc)
+        return pltpu.make_async_copy(up_ref.at[0, :, rows, :], lg.at[:, nb, c], l_loc.at[nb])
+
+    def blocks(o, body):
+        @pl.when(o != 1)
+        def _():
+            body(0)
+
+        @pl.when(o == 0)
+        def _():
+            body(1)
+
+    def others(body):
+        each(1, n_cols, lambda k: body((c + k) % n_cols))
+
+    def q_up(m):
+        return rcopy(pq.at[m], pin.at[m], q_send.at[m], q_recv.at[m], (r, 1))
+
+    def k_out(j, m):
+        return rcopy(ks.at[j, m], kd.at[c, m], k_send.at[j, m], k_recv.at[c, m], (r, j))
 
     def e_out(k):
         return rcopy(eb.at[c], eb.at[c], e_send.at[k], e_recv.at[c], (r, (c + k) % n_cols))
 
-    mine = pl.multiple_of(c * wc + q * wq, wq)
-    lz_own = pltpu.make_async_copy(up_ref.at[0, h, pl.ds(mine, wq), :], lz.at[c], lz_loc.at[0])
-    lz_own.start()
+    blocks(c, lambda nb: l_own(nb).start())
     barrier = pltpu.get_barrier_semaphore()
 
     def signal(dev):
@@ -464,40 +485,38 @@
 
         @pl.when(jnp.logical_and(active(i), q == t))
         def _():
-            nat_out(s, to_x, nat_x).start()
-            nat_out(s, to_y, nat_y).start()
+            nat_out(s).start()
+            for k in range(2):
+                nat_near(s, k).start()
             local_u(s).start()
 
     def lift_in(i):
         t, s = ts(i)
 
-        @pl.when(jnp.logical_and(active(i), c == 1))
+        @pl.when(lifted(i))
         def _():
             lift_full(t, s, q, lift_x, sib).wait_recv()
             lift_full(t, s, q, lift_x, to_x).start()
             lift_full(t, s, q, lift_y, to_y).start()
 
-    def relay(i):
+    def relay_native(i):
         t, s = ts(i)
 
-        @pl.when(active(i))
-        def _():
-            @pl.when(xn == t)
-            def _():
-                nat_full(t, s).wait_recv()
-                nat_half(t, s, 0, to_y).start()
-
-            @pl.when(yn == t)
-            def _():
-                nat_full(t, s).wait_recv()
-                nat_half(t, s, 1, to_x).start()
-
-            @pl.when(c == 1)
-            def _():
-                lift_full(t, s, xn, lift_x, sib).wait_recv()
-                lift_half(t, s, xn, 0, lift_fy, to_y).start()
-                lift_full(t, s, yn, lift_x, sib).wait_recv()
-                lift_half(t, s, yn, 1, lift_fx, to_x).start()
+        @pl.when(jnp.logical_and(active(i), yn == t))
+        def _():
+            for k in range(2):
+                nat_half(t, s, k, near1).wait_recv()
+                nat_half(t, s, k, half1).start()
+
+    def relay_lift(i):
+        t, s = ts(i)
+
+        @pl.when(lifted(i))
+        def _():
+            lift_full(t, s, xn, lift_x, sib).wait_recv()
+            lift_half(t, s, xn, 0, lift_fy, to_y).start()
+            lift_full(t, s, yn, lift_x, sib).wait_recv()
+            lift_half(t, s, yn, 1, lift_fx, to_x).start()
 
     def collect(i):
         t, s = ts(i)
@@ -506,55 +525,46 @@
         def _():
             @pl.when(dn == t)
             def _():
-                nat_half(t, s, 0, sib).wait_recv()
-                nat_half(t, s, 1, sib).wait_recv()
+                for k in range(2):
+                    nat_half(t, s, k, half1).wait_recv()
 
             @pl.when(q == t)
             def _():
                 local_u(s).wait()
 
+            @pl.when(xn == t)
+            def _():
+                nat_full(t, s).wait_recv()
+
             side(t, s, 1, 2 * t + h).start()
 
-            @pl.when(c == 1)
-            def _():
-                lift_half(t, s, dn, 0, lift_fy, sib).wait_recv()
-                lift_half(t, s, dn, 1, lift_fx, sib).wait_recv()
-                side(t, s, 0, 2 * t + h).start()
-
-    def pump(i):
-        @pl.when(i >= early)
-        def _():
-            lift_in(i)
-
-        relay(i)
-        native_out(i + 2)
-
-        @pl.when(i + 1 < early)
-        def _():
-            lift_in(i + 1)
-
-        collect(i)
-
-    def lifts():
-        for s in range(nsub):
-            each(0, chips, lambda g: lift_out(s, g).start())
-
-    @pl.when(jnp.logical_and(c == 0, q == chips - 1))
-    def _():
-        lifts()
-
-    @pl.when(c == 0)
-    def _():
-        x_up(0).start()
-
-    native_out(0)
-    native_out(1)
-    each(1, n_cols, lambda k: lz_out(k).start())
-
-    @pl.when(c == 0)
-    def _():
-        for m in range(1, tiles):
-            x_up(m).start()
+        @pl.when(lifted(i))
+        def _():
+            lift_half(t, s, dn, 0, lift_fy, sib).wait_recv()
+            lift_half(t, s, dn, 1, lift_fx, sib).wait_recv()
+            side(t, s, 0, 2 * t + h).start()
+
+    def lifts(s):
+        each(0, chips, lambda g: lift_out(s, g).start())
+
+    sender = jnp.where(c == 0, q > 1, jnp.logical_and(c == 1, q == 1))
+
+    @pl.when(sender)
+    def _():
+        lifts(0)
+
+    @pl.when(jnp.logical_and(sender, c == 1))
+    def _():
+        for s in range(1, nsub):
+            lifts(s)
+
+    @pl.when(c < 2)
+    def _():
+        for m in range(tiles):
+            x_swap(m).start()
+
+    each(0, stages, lambda i: pl.when(jnp.logical_or(c > 1, i < width))(lambda: native_out(i)))
+    others(lambda o: blocks(o, lambda nb: l_out(o, nb).start()))
 
     for m in range(tiles):
         for p in range(2):
@@ -572,62 +582,64 @@
     eb[c] = jnp.concatenate(parts, axis=0)
     each(1, n_cols, lambda k: e_out(k).start())
 
-    def spread():
-        lz_own.wait()
-        each(1, n_cols, lambda k: rcopy(
-            lz.at[(c + k) % n_cols], lz.at[(c + k) % n_cols], lz_send.at[k], lz_recv.at[(c + k) % n_cols], sib
-        ).wait_recv())
-        lg_side().start()
-        pltpu.make_async_copy(lz, lg.at[h, q], lg_loc.at[0]).start()
-        each(1, chips, lambda d: lg_out(d).start())
-
-    lift_in(0)
-
-    @pl.when(c == 1)
-    def _():
-        pump(0)
-
-    @pl.when(c != 1)
-    def _():
-        each(0, early, pump)
-
-    @pl.when(c == 0)
-    def _():
-        for m in range(tiles):
-            x_up(m).wait_send()
-
-            @pl.when(q == chips - 2 - m)
-            def _():
-                lifts()
-
-        @pl.when(jnp.logical_and(q > 0, q < chips - 1 - tiles))
-        def _():
-            lifts()
-
-    @pl.when(c != 1)
-    def _():
-        spread()
+    def spread(j):
+        def share(nb):
+            p = l_part(j, nb, q)
+            rcopy(p, p, l_send.at[j, nb], l_recv.at[j, nb], sib).wait_recv()
+            each(1, chips, lambda d: g_out(j, nb, d).start())
+
+        blocks(c, share)
+
+    @pl.when(c < 2)
+    def _():
+        for i in range(width):
+            lift_in(i)
+        for i in range(width):
+            relay_native(i)
+            relay_lift(i)
+        for i in range(width, stages):
+            native_out(i)
+
+        @pl.when(c == 0)
+        def _():
+            x_swap(0).wait_send()
+
+            @pl.when(sender)
+            def _():
+                for s in range(1, nsub):
+                    lifts(s)
+
+        for i in range(width, stages):
+            lift_in(i)
+        for i in range(width):
+            collect(i)
+
+    @pl.when(c > 1)
+    def _():
+        each(0, stages, relay_native)
+        each(0, stages, collect)
+        others(spread)
 
     def gather():
-        def pass_on(d):
-            o = ahead(d)
-            rcopy(lz, lg.at[h, o], lg_send.at[d], lg_recv.at[h, o], sib).wait_recv()
-            lg_forward(d).start()
-
-        each(1, chips, pass_on)
+        blocks(c, lambda nb: l_own(nb).wait())
+
+        def pieces(j, nb):
+            def got(d):
+                p = l_part(j, nb, ahead(d))
+                rcopy(p, p, g_send.at[j, nb, d], g_recv.at[j, nb, ahead(d)], sib).wait_recv()
+
+            each(1, chips, got)
+            l_sib(j, nb, h).start()
+
+        others(lambda j: blocks(c, lambda nb: pieces(j, nb)))
+        others(lambda j: blocks(c, lambda nb: l_sib(j, nb, 1 - h).wait_recv()))
+
+    def entries_in():
         each(1, n_cols, lambda k: rcopy(
             eb.at[(c + k) % n_cols], eb.at[(c + k) % n_cols], e_send.at[k], e_recv.at[(c + k) % n_cols], sib
         ).wait_recv())
-        pltpu.make_async_copy(lz, lg.at[h, q], lg_loc.at[0]).wait()
-        each(0, chips, lambda o: rcopy(
-            lz, lg.at[1 - h, o], lg_sib.at[0], lg_recv.at[1 - h, o], sib
-        ).wait_recv())
-
-    def finish(m):
-        @pl.when(m == 0)
-        def _():
-            gather()
-
+
+    def scaled(t, m, nb):
         entries = jnp.sum(eb[...], axis=0)
         lines = []
         levels = lax.broadcasted_iota(jnp.int32, (1, ranks), 1)
@@ -647,58 +659,85 @@
         vr, vi = [], []
         for hh in range(2):
             for s in range(nsub):
-                vr.append(ps[2 * c + hh, s, m, 0])
-                vi.append(ps[2 * c + hh, s, m, 1])
+                vr.append(ps[2 * t + hh, s, m, 0])
+                vi.append(ps[2 * t + hh, s, m, 1])
         vr, vi = jnp.concatenate(vr, axis=1), jnp.concatenate(vi, axis=1)
         wr = vr * fr - vi * fi
         wi = vr * fi + vi * fr
+        a, b = split(wr)
+        ch[nb, m, 0:ranks, :] = a
+        cl[nb, m, 0:ranks, :] = b
+        a, b = split(wi)
+        ch[nb, m, ranks:2 * ranks, :] = a
+        cl[nb, m, ranks:2 * ranks, :] = b
+        return wr, wi
+
+    def finish_next(m):
+        @pl.when(m == 0)
+        def _():
+            entries_in()
+
+        wr, wi = scaled(c + 1, m, 1)
+        pq[m, 0] = wr
+        pq[m, 1] = wi
+        q_up(m).start()
+
+    def finish(m):
+        @pl.when(m == 0)
+        def _():
+            gather()
+
+            @pl.when(c > 0)
+            def _():
+                entries_in()
+
+        wr, wi = scaled(c, m, 0)
         panel_ref[m, 0] = wr
         panel_ref[m, 1] = wi
-        a, b = split(wr)
-        ch[0:ranks, :] = a
-        cl[0:ranks, :] = b
-        a, b = split(wi)
-        ch[ranks:2 * ranks, :] = a
-        cl[ranks:2 * ranks, :] = b
 
         def core(j, carry):
-            rank2 = lz.shape[2]
-            lr = lg[0, :, j].reshape(wc, rank2)
-            li = lg[1, :, j].reshape(wc, rank2)
-            uh, ul = split(jnp.concatenate([lr, li], axis=1))
-            prod = dot3(ch[...], cl[...], uh, ul)
-            ks[j, m, 0] = prod[:ranks, :rank2] - prod[ranks:, rank2:]
-            ks[j, m, 1] = prod[:ranks, rank2:] + prod[ranks:, :rank2]
-
-            @pl.when(j < c)
-            def _():
-                k_down(j, m).start()
-
-            @pl.when(jnp.logical_and(c == 0, j > 0))
-            def _():
-                k_up(j, m).start()
+            def product(nb):
+                uh, ul = split(jnp.concatenate([lg[0, nb, j], lg[1, nb, j]], axis=1))
+                prod = dot3(ch[nb, m], cl[nb, m], uh, ul)
+                real = prod[:ranks, :rank2] - prod[ranks:, rank2:]
+                imag = prod[:ranks, rank2:] + prod[ranks:, :rank2]
+                return real, imag
+
+            real, imag = product(0)
+
+            @pl.when(c > 0)
+            def _():
+                ks[j, m, 0] = real
+                ks[j, m, 1] = imag
+
+            @pl.when(c == 0)
+            def _():
+                real1, imag1 = product(1)
+                ks[j, m, 0] = real + real1
+                ks[j, m, 1] = imag + imag1
+
+            @pl.when(j != c)
+            def _():
+                k_out(j, m).start()
 
             return carry
 
         lax.fori_loop(0, n_cols, core, 0)
 
-    head = early * tiles
-    tail = stages - early
-    total = head + tail * tiles
-    first_final = jnp.where(c == 0, nsub, (n_cols - c) * nsub)
-    final0 = jnp.where(c == 1, head + tail - 1, first_final - 1)
-    final1 = jnp.where(c == 1, tail, early)
+    half = width * tiles
+    total = 2 * half
+    final0 = jnp.where(c == 0, half + nsub - 1, (nsub - 1) * half + n_cols - 1 - c)
 
     def unit(u, carry):
-        i = jnp.where(u < head, u % early, early + (u - head) % tail)
-        m = jnp.where(u < head, u // early, (u - head) // tail)
+        i = u // half * width + u % width
+        m = u // width % tiles
         t, s = ts(i)
 
         @pl.when(active(i))
         def _():
-            @pl.when(jnp.logical_and(c == 1, jnp.logical_and(u < head, u % early == 0)))
-            def _():
-                x_up(m).wait_recv()
+            @pl.when(jnp.logical_and(c < 2, jnp.logical_and(u < half, u % width == 0)))
+            def _():
+                x_swap(m).wait_recv()
                 for p in range(2):
                     a, b = split(x0[m, p])
                     xh[0, m, p * ranks:(p + 1) * ranks, :] = a
@@ -712,7 +751,7 @@
                     def _():
                         side(t, s, 1, b).wait_recv()
 
-                        @pl.when(c == 1)
+                        @pl.when(lifted(i))
                         def _():
                             side(t, s, 0, b).wait_recv()
 
@@ -725,13 +764,13 @@
 
                 real, imag = product(1)
 
-                @pl.when(c == 1)
+                @pl.when(lifted(i))
                 def _():
                     real0, imag0 = product(0)
                     ps[b, s, m, 0] = real + real0
                     ps[b, s, m, 1] = imag + imag0
 
-                @pl.when(c == 0)
+                @pl.when(jnp.logical_and(c == 0, t == 0))
                 def _():
                     ps[b, s, m, 0] = real
                     ps[b, s, m, 1] = imag
@@ -742,59 +781,78 @@
                     ps[b, s, m, 0] = real + pr[b, s, m, 0]
                     ps[b, s, m, 1] = imag + pr[b, s, m, 1]
 
-                @pl.when(t > c)
+                @pl.when(jnp.logical_and(t > c, c > 0))
                 def _():
                     p_up(b, s, m).start()
 
-        @pl.when(jnp.logical_or(u == final0, u == final0 + final1))
+        @pl.when(jnp.logical_and(c == 0, jnp.logical_and(u < half, u % width == width - 1)))
+        def _():
+            finish_next(m)
+
+        @pl.when(jnp.logical_and(c != 1, jnp.logical_or(u == final0, u == final0 + width)))
         def _():
             finish(m)
 
+        @pl.when(jnp.logical_and(c < 2, u == width - 1))
+        def _():
+            for i in range(width, stages):
+                relay_native(i)
+                relay_lift(i)
+
+        @pl.when(jnp.logical_and(c < 2, u == half - 1))
+        def _():
+            for i in range(width, stages):
+                collect(i)
+
+            @pl.when(c == 0)
+            def _():
+                others(spread)
+
+        return carry
+
+    lax.fori_loop(0, total, unit, 0)
+
+    @pl.when(c == 1)
+    def _():
+        entries_in()
+        for m in range(tiles):
+            q_up(m).wait_recv()
+            panel_ref[m] = pin[m]
+
+    for m in range(tiles):
+        @pl.when(c != 1)
+        def _():
+            cores_ref[m, 0] = ks[c, m]
+
         @pl.when(c == 1)
         def _():
-            @pl.when(u + 1 < early)
-            def _():
-                pump(u + 1)
-
-            @pl.when(u == early - 1)
-            def _():
-                spread()
-
-            @pl.when(jnp.logical_and(u >= early + 1, u < early + 1 + tail))
-            def _():
-                pump(u - 1)
-
-        return carry
-
-    lax.fori_loop(0, total, unit, 0)
-
-    @pl.when(c > 0)
-    def _():
-        for m in range(tiles):
-            def lower(j):
-                k_up(j, m).wait_recv()
-                ks[j, m] = ks[j, m] + ku[j, m]
-
-                @pl.when(j > c)
-                def _():
-                    k_up(j, m).start()
-
-            each(c, n_cols, lower)
-
-    for m in range(tiles):
-        cores_ref[m, 0] = ks[c, m]
-
-        def upper(o):
-            rcopy(ks.at[c, m], kd.at[o, m], kd_send.at[c, m], kd_recv.at[o, m], sib).wait_recv()
-            cores_ref[m, 0] = cores_ref[m, 0] + kd[o, m]
-
-        each(c + 1, n_cols, upper)
-
-    @pl.when(jnp.logical_and(c == 0, q > 0))
+            cores_ref[m, 0] = jnp.zeros_like(ks[c, m])
+
+        def add(o):
+            @pl.when(o != 1)
+            def _():
+                rcopy(ks.at[c, m], kd.at[o, m], k_send.at[c, m], k_recv.at[o, m], sib).wait_recv()
+                cores_ref[m, 0] = cores_ref[m, 0] + kd[o, m]
+
+        others(add)
+
+    @pl.when(sender)
     def _():
         for s in range(nsub):
             each(0, chips, lambda g: lift_out(s, g).wait_send())
 
+    @pl.when(c < 2)
+    def _():
+        for m in range(tiles):
+            @pl.when(jnp.logical_or(c == 1, m > 0))
+            def _():
+                x_swap(m).wait_send()
+
+    @pl.when(c == 0)
+    def _():
+        for m in range(tiles):
+            q_up(m).wait_send()
+
     def drain(i):
         t, s = ts(i)
 
@@ -802,16 +860,18 @@
         def _():
             @pl.when(q == t)
             def _():
-                nat_out(s, to_x, nat_x).wait_send()
-                nat_out(s, to_y, nat_y).wait_send()
-
-            @pl.when(jnp.logical_or(xn == t, yn == t))
-            def _():
-                nat_half(t, s, 0, sib).wait_send()
+                nat_out(s).wait_send()
+                for k in range(2):
+                    nat_near(s, k).wait_send()
+
+            @pl.when(yn == t)
+            def _():
+                for k in range(2):
+                    nat_half(t, s, k, half1).wait_send()
 
             side(t, s, 1, 2 * t + h).wait_send()
 
-            @pl.when(c == 1)
+            @pl.when(lifted(i))
             def _():
                 lift_full(t, s, q, lift_x, sib).wait_send()
                 lift_full(t, s, q, lift_y, sib).wait_send()
@@ -819,7 +879,7 @@
                 lift_half(t, s, yn, 1, lift_fx, sib).wait_send()
                 side(t, s, 0, 2 * t + h).wait_send()
 
-            @pl.when(t > c)
+            @pl.when(jnp.logical_and(t > c, c > 0))
             def _():
                 for m in range(tiles):
                     for e in range(2):
@@ -827,21 +887,21 @@
 
     each(0, stages, drain)
 
-    def tail_l(d):
-        lg_out(d).wait_send()
-        lg_forward(d).wait_send()
-
-    each(1, chips, tail_l)
-    lg_side().wait_send()
-
-    def tail_z(k):
-        lz_out(k).wait_send()
-        e_out(k).wait_send()
-
-    each(1, n_cols, tail_z)
-    for m in range(tiles):
-        each(0, c, lambda j: k_down(j, m).wait_send())
-        each(c + 1, n_cols, lambda j: k_up(j, m).wait_send())
+    def tail_l(j):
+        def left(nb):
+            each(1, chips, lambda d: g_out(j, nb, d).wait_send())
+            l_sib(j, nb, h).wait_send()
+
+        blocks(c, left)
+        blocks(j, lambda nb: l_out(j, nb).wait_send())
+
+        @pl.when(c != 1)
+        def _():
+            for m in range(tiles):
+                k_out(j, m).wait_send()
+
+    others(tail_l)
+    each(1, n_cols, lambda k: e_out(k).wait_send())
 
 
 def paired(n_rows, n_cols, col_samples, row_samples, pivot_rows, rank_blocks, upper_inverse, upanel_left):
@@ -851,7 +911,6 @@
     chips = n_rows // 2
     nsub = wr // 128
     sw = wr // nsub
-    wq = wc // chips
     f32, bf16 = jnp.float32, jnp.bfloat16
     dma = pltpu.SemaphoreType.DMA
     vmem = pl.BlockSpec(memory_space=pltpu.VMEM)
@@ -869,27 +928,26 @@
             pltpu.VMEM((2, tiles, 2 * ranks, wc), bf16),
             pltpu.VMEM((2, tiles, 2 * ranks, wc), bf16),
             pltpu.VMEM((tiles, 2, ranks, wc), f32),
-            pltpu.VMEM((2 * ranks, wc), bf16),
-            pltpu.VMEM((2 * ranks, wc), bf16),
+            pltpu.VMEM((2, tiles, 2 * ranks, wc), bf16),
+            pltpu.VMEM((2, tiles, 2 * ranks, wc), bf16),
             pltpu.VMEM((n_rows, nsub, 2, 2, wc, sw), f32),
             sums,
             sums,
-            pltpu.VMEM((n_cols, wq, left_ranks), f32),
-            pltpu.VMEM((2, chips, n_cols, wq, left_ranks), f32),
-            pltpu.VMEM((n_cols, tiles, 2, ranks, left_ranks), f32),
+            pltpu.VMEM((tiles, 2, ranks, wc), f32),
+            pltpu.VMEM((tiles, 2, ranks, wc), f32),
+            pltpu.VMEM((2, 2, n_cols, wc, left_ranks), f32),
             pltpu.VMEM((n_cols, tiles, 2, ranks, left_ranks), f32),
             pltpu.VMEM((n_cols, tiles, 2, ranks, left_ranks), f32),
             pltpu.VMEM((n_cols, -(-2 * tiles // 8) * 8, ranks), f32),
-            dma((nsub,)), dma((nsub,)), dma((nsub,)), dma((n_cols, nsub)), dma((n_cols, nsub)),
-            dma((n_cols, nsub, 2)),
+            dma((nsub,)), dma((nsub,)), dma((nsub, 2)), dma((n_cols, nsub, 2)), dma((n_cols, nsub)),
+            dma((n_cols, nsub, 2)), dma((n_cols, nsub, 2)),
             dma((nsub, chips)), dma((n_cols, nsub, chips)), dma((n_cols, nsub, 2)),
             dma((n_cols, nsub)), dma((n_cols, nsub)), dma((n_cols, nsub)), dma((n_cols, nsub)),
             dma((n_cols, nsub, 2)), dma((n_cols, nsub, 2)), dma((tiles,)), dma((tiles,)),
-            dma((n_rows, nsub, tiles)), dma((n_rows, nsub, tiles)),
-            dma((1,)), dma((n_cols,)), dma((n_cols,)), dma((1,)), dma((chips,)), dma((1,)), dma((chips,)),
-            dma((2, chips)),
-            dma((n_cols, tiles)), dma((n_cols, tiles)), dma((n_cols, tiles)), dma((n_cols, tiles)),
-            dma((n_cols,)), dma((n_cols,)),
+            dma((n_rows, nsub, tiles)), dma((n_rows, nsub, tiles)), dma((tiles,)), dma((tiles,)),
+            dma((2,)), dma((n_cols, 2)), dma((n_cols, 2)), dma((n_cols, 2, chips)), dma((n_cols, 2, chips)),
+            dma((n_cols, 2)), dma((n_cols, 2)),
+            dma((n_cols, tiles)), dma((n_cols, tiles)), dma((n_cols,)), dma((n_cols,)),
         ],
         compiler_params=pltpu.CompilerParams(
             collective_id=0, has_side_effects=True, vmem_limit_bytes=56 * 1024 * 1024
@@ -904,7 +962,7 @@
     chips = n_rows // 2
     if chips != n_cols or wc != 2 * wr:
         raise ValueError("unsupported mesh")
-    if chips == 4 and wr % 128 == 0:
+    if chips == 4 and wr == 128 * (n_cols - 2):
         return paired(
             n_rows, n_cols, col_samples, row_samples, pivot_rows, rank_blocks, upper_inverse, upanel_left
         )

time: 172 us -> 140 us (0.81)
  Pallas kernels: 168 us -> 134 us
    pallas_call x1, Pallas kernels: 168 us -> 134 us  [paired(): pl.pallas_call(functools.partial(paired_kernel, n_rows, n_cols), out_shap...]
where the time goes in v2:
time: 140 us; the launch traced here: 138 us
  Pallas kernels  134 us (96%)
  local copies, waits for them, and re-layouts  3.01 us (2%)
    pallas_call x1, Pallas kernels, paired(): pl.pallas_call(functools.partial(paired_kernel, n_rows, n_cols), out_shap...  134 us
    unnamed x4, local copies, waits for them, and re-layouts  3.01 us

profile of v2, /device:TPU:28, one launch (start us, length us, event | category | flops | bytes accessed | tf_op | source)
XLA Modules:
  0.0 137.7 jit_solution(2184833040666657278)
XLA Ops:
  0.6 134.1 %shard_map.77 = (f32[2,2,128,512]{3,2,1,0:T(8,128)}, f32[2,1,2,128,128]{4,3,2,1,0:T(8,128)}) custom-call(f32[2,2,128,512]{3,2,1,0:T(8,128)} %row_ref.1, f32[2,512,256]{2,1,0:T(8,128)} %u_ref.1, f32[1,2,2048,128]{3,2,1,0:T(8,128)} %up_ref.1, f32[2,2,512,128]{3,2,1,0:T(8,128)} %col_ref.1, s32[2,128]{1,0:T(2,128)} %piv_ref.1, s32[2]{0:T(128)} %rank_ref.1), custom_call_target="tpu_custom_call" | custom-call | tf_op jit(solution)/shard_map/pallas_call | solution.py:919
  134.7 0.0 copy-start
  134.7 2.3 %copy.10 = f32[2,2,128,512]{3,2,1,0:T(8,128)} copy(f32[2,2,128,512]{3,2,1,0:T(8,128)} %get-tuple-element.4) | data formatting | bytes 2097152
  137.0 0.0 copy-done
  137.0 0.7 copy.11
Async XLA Ops:
  134.7 2.3 %copy-start = (f32[2,1,2,128,128]{4,3,2,1,0:T(8,128)S(1)}, f32[2,1,2,128,128]{4,3,2,1,0:T(8,128)}, u32[]{:S(2)}) copy-start(f32[2,1,2,128,128]{4,3,2,1,0:T(8,128)} %get-tuple-element.5) | copy-start | bytes 786436

commit v3 on v2

--- a/solution.py
+++ b/solution.py
@@ -330,16 +330,23 @@
     each(1, n_cols, tail)
 
 
+def stacked(x, uh, ul):
+    rows = x.shape[0] // 2
+    high = jnp.dot(x, uh, preferred_element_type=jnp.float32)
+    low = jnp.dot(x[:rows], ul, preferred_element_type=jnp.float32)
+    return high[:rows] + (high[rows:] + low)
+
+
 def paired_kernel(
     n_rows, n_cols,
     row_ref, u_ref, up_ref, col_ref, piv_ref, rank_ref,
     panel_ref, cores_ref,
-    xh, xl, x0, ch, cl, us, ps, pr, pq, pin, lg, ks, kd, eb,
+    xs, x0, cs, us, uc, lc, stg, ps, pr, pq, pin, lg, ks, ku, kd, eb,
     u_loc, nat_x, nat_y, nat_fwd, full1, near1, half1,
-    lift, full0, half0, lift_x, lift_y, lift_fx, lift_fy,
+    lift, sc_send, sc_recv, full0, half0, lift_x, lift_y, lift_fx, lift_fy,
     side_send, side_recv, x_send, x_recv, p_send, p_recv, q_send, q_recv,
     l_loc, l_send, l_recv, g_send, g_recv, l_side, l_got,
-    k_send, k_recv, e_send, e_recv,
+    k_send, ku_recv, k_recv, e_send, e_recv,
 ):
     r, c = lax.axis_index("row"), lax.axis_index("col")
     chips = n_rows // 2
@@ -350,7 +357,7 @@
     tiles, _, ranks, wc = row_ref.shape
     nsub, sw = us.shape[1], us.shape[5]
     wq = wc // chips
-    rank2 = lg.shape[4]
+    rank2 = lg.shape[3]
     width = n_cols - 2
     sib = (q * 2 + 1 - h, c)
     to_x, to_y = (xn * 2 + h, c), (yn * 2 + h, c)
@@ -395,17 +402,23 @@
         b = 2 * t + h
         return rcopy(us.at[b, s, 1], us.at[b, s, 1], nat_fwd.at[t, s, 0], full1.at[t, s], sib)
 
-    def nat_half(t, s, k, got):
+    def nat_half(t, s, k, got, dev=None):
         part = us.at[2 * t + h, s, 1, :, k * (wc // 2):(k + 1) * (wc // 2), :]
-        return rcopy(part, part, nat_fwd.at[t, s, k], got.at[t, s, k], to_x)
+        return rcopy(part, part, nat_fwd.at[t, s, k], got.at[t, s, k], dev or to_x)
 
     def piece(b, s, g):
         return us.at[b, s, 0, :, pl.ds(pl.multiple_of(g * wq, wq), wq), :]
 
-    def lift_out(s, g):
+    def upiece(s, g):
         rows = pl.ds(pl.multiple_of(g * wq, wq), wq)
-        src = u_ref.at[:, rows, pl.ds(pl.multiple_of(s * sw, sw), sw)]
-        return rcopy(src, piece(r, s, g), lift.at[s, g], full0.at[q, s, g], (g * 2 + h, 1 - c))
+        return u_ref.at[:, rows, pl.ds(pl.multiple_of(s * sw, sw), sw)]
+
+    def scatter(s, g):
+        slot = stg.at[q % width, s]
+        return rcopy(upiece(s, g), slot, sc_send.at[s, g], sc_recv.at[q % width, s], (g * 2 + h, c))
+
+    def raised(t, s, src):
+        return rcopy(src, piece(2 * t + h, s, q), lift.at[s, t], full0.at[t, s, q], (r, 1 - c))
 
     def lift_full(t, s, g, sem, dev):
         p = piece(2 * t + h, s, g)
@@ -419,38 +432,32 @@
     def side(t, s, kk, b):
         return rcopy(us.at[b, s, kk], us.at[b, s, kk], side_send.at[t, s, kk], side_recv.at[t, s, kk], sib)
 
-    def x_swap(m):
-        return rcopy(row_ref.at[m], x0.at[m], x_send.at[m], x_recv.at[m], (r, 1 - c))
+    def x_swap(m, p):
+        return rcopy(row_ref.at[m, p], x0.at[m, p], x_send.at[m, p], x_recv.at[m, p], (r, 1 - c))
 
     def p_up(b, s, m):
         return rcopy(ps.at[b, s, m], pr.at[b, s, m], p_send.at[b, s, m], p_recv.at[b, s, m], (r, c + 1))
 
-    def l_part(j, nb, g):
-        return lg.at[h, nb, j, pl.ds(pl.multiple_of(g * wq, wq), wq), :]
-
-    def l_out(o, nb):
-        rows = pl.ds(pl.multiple_of((o + nb) * wc + q * wq, wq), wq)
-        return rcopy(up_ref.at[0, h, rows, :], l_part(c, nb, q), l_send.at[o, nb], l_recv.at[c, nb], (r, o))
-
-    def g_out(j, nb, d):
-        p = l_part(j, nb, q)
-        return rcopy(p, p, g_send.at[j, nb, d], g_recv.at[j, nb, q], (ahead(d) * 2 + h, c))
-
-    def l_sib(j, nb, comp):
-        return rcopy(lg.at[comp, nb, j], lg.at[comp, nb, j], l_side.at[j, nb], l_got.at[j, nb], sib)
-
-    def l_own(nb):
-        rows = pl.ds(pl.multiple_of((c + nb) * wc, wc), wc)
-        return pltpu.make_async_copy(up_ref.at[0, :, rows, :], lg.at[:, nb, c], l_loc.at[nb])
-
-    def blocks(o, body):
-        @pl.when(o != 1)
-        def _():
-            body(0)
-
-        @pl.when(o == 0)
-        def _():
-            body(1)
+    def l_down(o):
+        rows = pl.ds(pl.multiple_of(o * wc, wc), wc)
+        return rcopy(up_ref.at[0, h, rows, :], lg.at[h, c], l_send.at[o], l_recv.at[c], (r, o))
+
+    def l_part(j, g):
+        return lg.at[h, j, pl.ds(pl.multiple_of(g * wq, wq), wq), :]
+
+    def l_up(o):
+        rows = pl.ds(pl.multiple_of(o * wc + q * wq, wq), wq)
+        return rcopy(up_ref.at[0, h, rows, :], l_part(c, q), l_send.at[o], l_recv.at[c], (r, o))
+
+    def g_out(j, d):
+        return rcopy(l_part(j, q), l_part(j, q), g_send.at[j, d], g_recv.at[j, q], (ahead(d) * 2 + h, c))
+
+    def l_sib(j, comp):
+        return rcopy(lg.at[comp, j], lg.at[comp, j], l_side.at[j], l_got.at[j], sib)
+
+    def l_own():
+        rows = pl.ds(pl.multiple_of(c * wc, wc), wc)
+        return pltpu.make_async_copy(up_ref.at[0, :, rows, :], lg.at[:, c], l_loc.at[0])
 
     def others(body):
         each(1, n_cols, lambda k: body((c + k) % n_cols))
@@ -461,10 +468,13 @@
     def k_out(j, m):
         return rcopy(ks.at[j, m], kd.at[c, m], k_send.at[j, m], k_recv.at[c, m], (r, j))
 
+    def k_next(j, m):
+        return rcopy(ks.at[j, m], ku.at[j, m], k_send.at[j, m], ku_recv.at[j, m], (r, 1))
+
     def e_out(k):
         return rcopy(eb.at[c], eb.at[c], e_send.at[k], e_recv.at[c], (r, (c + k) % n_cols))
 
-    blocks(c, lambda nb: l_own(nb).start())
+    l_own().start()
     barrier = pltpu.get_barrier_semaphore()
 
     def signal(dev):
@@ -480,15 +490,25 @@
 
     pl.semaphore_wait(barrier, 1 + (chips - 1) + (n_cols - 1) + jnp.where(c < 2, chips - 1, 0))
 
-    def native_out(i):
+    def native_x(i):
         t, s = ts(i)
 
         @pl.when(jnp.logical_and(active(i), q == t))
         def _():
             nat_out(s).start()
+            local_u(s).start()
+
+    def native_y(i):
+        t, s = ts(i)
+
+        @pl.when(jnp.logical_and(active(i), q == t))
+        def _():
             for k in range(2):
                 nat_near(s, k).start()
-            local_u(s).start()
+
+    def native_out(i):
+        native_x(i)
+        native_y(i)
 
     def lift_in(i):
         t, s = ts(i)
@@ -504,9 +524,19 @@
 
         @pl.when(jnp.logical_and(active(i), yn == t))
         def _():
-            for k in range(2):
-                nat_half(t, s, k, near1).wait_recv()
-                nat_half(t, s, k, half1).start()
+            nat_half(t, s, 0, near1).wait_recv()
+
+            @pl.when(c > 0)
+            def _():
+                nat_half(t, s, 0, half1).start()
+
+            nat_half(t, s, 1, near1).wait_recv()
+            nat_half(t, s, 1, half1).start()
+
+        @pl.when(jnp.logical_and(c == 0, xn == t))
+        def _():
+            nat_full(t, s).wait_recv()
+            nat_half(t, s, 0, half1, to_y).start()
 
     def relay_lift(i):
         t, s = ts(i)
@@ -532,7 +562,7 @@
             def _():
                 local_u(s).wait()
 
-            @pl.when(xn == t)
+            @pl.when(jnp.logical_and(c > 0, xn == t))
             def _():
                 nat_full(t, s).wait_recv()
 
@@ -544,33 +574,48 @@
             lift_half(t, s, dn, 1, lift_fx, sib).wait_recv()
             side(t, s, 0, 2 * t + h).start()
 
-    def lifts(s):
-        each(0, chips, lambda g: lift_out(s, g).start())
-
-    sender = jnp.where(c == 0, q > 1, jnp.logical_and(c == 1, q == 1))
-
-    @pl.when(sender)
+    source = jnp.where(c == 0, q > 1, jnp.logical_and(c == 1, q == 1))
+
+    def scatters(s):
+        @pl.when(source)
+        def _():
+            each(1, chips, lambda d: scatter(s, ahead(d)).start())
+
+    for s in range(nsub):
+        scatters(s)
+
+    each(0, stages, lambda i: pl.when(jnp.logical_or(c > 1, i < width))(lambda: native_out(i)))
+    def climb(t, s):
+        @pl.when(q == t)
+        def _():
+            raised(t, s, upiece(s, q)).start()
+
+        @pl.when(q != t)
+        def _():
+            rcopy(stg.at[t % width, s], stg.at[t % width, s], lift.at[s, t], sc_recv.at[t % width, s], sib).wait_recv()
+            raised(t, s, stg.at[t % width, s]).start()
+
+    @pl.when(c == 0)
     def _():
-        lifts(0)
-
-    @pl.when(jnp.logical_and(sender, c == 1))
+        for s in range(nsub):
+            for t in range(n_cols - 1, 1, -1):
+                climb(t, s)
+            for p in range(2):
+                x_swap(s, p).start()
+
+    @pl.when(c == 1)
     def _():
-        for s in range(1, nsub):
-            lifts(s)
-
-    @pl.when(c < 2)
+        for s in range(nsub):
+            climb(1, s)
+        for m in range(tiles):
+            for p in range(2):
+                x_swap(m, p).start()
+
+    each(c + 1, n_cols, lambda o: l_up(o).start())
+
+    @pl.when(c == 1)
     def _():
-        for m in range(tiles):
-            x_swap(m).start()
-
-    each(0, stages, lambda i: pl.when(jnp.logical_or(c > 1, i < width))(lambda: native_out(i)))
-    others(lambda o: blocks(o, lambda nb: l_out(o, nb).start()))
-
-    for m in range(tiles):
-        for p in range(2):
-            a, b = split(row_ref[m, p])
-            xh[1, m, p * ranks:(p + 1) * ranks, :] = a
-            xl[1, m, p * ranks:(p + 1) * ranks, :] = b
+        l_down(0).start()
 
     pos = c * wc + lax.broadcasted_iota(jnp.int32, (wc, ranks), 0)
     parts = []
@@ -583,63 +628,84 @@
     each(1, n_cols, lambda k: e_out(k).start())
 
     def spread(j):
-        def share(nb):
-            p = l_part(j, nb, q)
-            rcopy(p, p, l_send.at[j, nb], l_recv.at[j, nb], sib).wait_recv()
-            each(1, chips, lambda d: g_out(j, nb, d).start())
-
-        blocks(c, share)
+        rcopy(l_part(j, q), l_part(j, q), l_send.at[c], l_recv.at[j], sib).wait_recv()
+        each(1, chips, lambda d: g_out(j, d).start())
 
     @pl.when(c < 2)
     def _():
         for i in range(width):
             lift_in(i)
-        for i in range(width):
-            relay_native(i)
-            relay_lift(i)
-        for i in range(width, stages):
-            native_out(i)
+
+            @pl.when(c == 0)
+            def _():
+                native_x(width + i)
+
+        relay_native(0)
+
+        @pl.when(c == 1)
+        def _():
+            relay_lift(0)
 
         @pl.when(c == 0)
         def _():
-            x_swap(0).wait_send()
-
-            @pl.when(sender)
-            def _():
-                for s in range(1, nsub):
-                    lifts(s)
-
-        for i in range(width, stages):
-            lift_in(i)
+            native_y(width)
+            relay_lift(0)
+            relay_lift(1)
+            relay_native(1)
+            for i in range(width + 1, stages):
+                native_y(i)
+
+        @pl.when(c == 1)
+        def _():
+            for i in range(1, width):
+                relay_native(i)
+                relay_lift(i)
+            for i in range(width, stages):
+                native_out(i)
+
         for i in range(width):
             collect(i)
 
     @pl.when(c > 1)
     def _():
         each(0, stages, relay_native)
+        each(0, c, lambda o: l_down(o).start())
         each(0, stages, collect)
-        others(spread)
+        each(0, c, spread)
+
+
+    for m in range(tiles):
+        for p in range(2):
+            a, b = split(row_ref[m, p])
+            xs[1, m, p * ranks:(p + 1) * ranks, :] = a
+            xs[1, m, (p + 2) * ranks:(p + 3) * ranks, :] = b
 
     def gather():
-        blocks(c, lambda nb: l_own(nb).wait())
-
-        def pieces(j, nb):
-            def got(d):
-                p = l_part(j, nb, ahead(d))
-                rcopy(p, p, g_send.at[j, nb, d], g_recv.at[j, nb, ahead(d)], sib).wait_recv()
-
-            each(1, chips, got)
-            l_sib(j, nb, h).start()
-
-        others(lambda j: blocks(c, lambda nb: pieces(j, nb)))
-        others(lambda j: blocks(c, lambda nb: l_sib(j, nb, 1 - h).wait_recv()))
+        l_own().wait()
+
+        def low(j):
+            each(1, chips, lambda d: rcopy(
+                l_part(j, ahead(d)), l_part(j, ahead(d)), g_send.at[j, d], g_recv.at[j, ahead(d)], sib
+            ).wait_recv())
+            l_sib(j, h).start()
+
+        def high(j):
+            rcopy(lg.at[h, j], lg.at[h, j], l_send.at[c], l_recv.at[j], sib).wait_recv()
+            l_sib(j, h).start()
+
+        each(0, c, low)
+        each(c + 1, n_cols, high)
+
+    def gathered():
+        each(0, c, lambda j: l_sib(j, 1 - h).wait_recv())
+        each(c + 1, n_cols, lambda j: l_sib(j, 1 - h).wait_recv())
 
     def entries_in():
         each(1, n_cols, lambda k: rcopy(
             eb.at[(c + k) % n_cols], eb.at[(c + k) % n_cols], e_send.at[k], e_recv.at[(c + k) % n_cols], sib
         ).wait_recv())
 
-    def scaled(t, m, nb):
+    def scaled(t, m):
         entries = jnp.sum(eb[...], axis=0)
         lines = []
         levels = lax.broadcasted_iota(jnp.int32, (1, ranks), 1)
@@ -664,12 +730,6 @@
         vr, vi = jnp.concatenate(vr, axis=1), jnp.concatenate(vi, axis=1)
         wr = vr * fr - vi * fi
         wi = vr * fi + vi * fr
-        a, b = split(wr)
-        ch[nb, m, 0:ranks, :] = a
-        cl[nb, m, 0:ranks, :] = b
-        a, b = split(wi)
-        ch[nb, m, ranks:2 * ranks, :] = a
-        cl[nb, m, ranks:2 * ranks, :] = b
         return wr, wi
 
     def finish_next(m):
@@ -677,7 +737,7 @@
         def _():
             entries_in()
 
-        wr, wi = scaled(c + 1, m, 1)
+        wr, wi = scaled(c + 1, m)
         pq[m, 0] = wr
         pq[m, 1] = wi
         q_up(m).start()
@@ -685,38 +745,50 @@
     def finish(m):
         @pl.when(m == 0)
         def _():
-            gather()
+            gathered()
 
             @pl.when(c > 0)
             def _():
                 entries_in()
 
-        wr, wi = scaled(c, m, 0)
-        panel_ref[m, 0] = wr
-        panel_ref[m, 1] = wi
+        @pl.when(c == 1)
+        def _():
+            q_up(m).wait_recv()
+            panel_ref[m] = pin[m]
+
+        @pl.when(c != 1)
+        def _():
+            wr, wi = scaled(c, m)
+            panel_ref[m, 0] = wr
+            panel_ref[m, 1] = wi
+
+        for p in range(2):
+            a, b = split(panel_ref[m, p])
+            cs[p * ranks:(p + 1) * ranks, :] = a
+            cs[(p + 2) * ranks:(p + 3) * ranks, :] = b
 
         def core(j, carry):
-            def product(nb):
-                uh, ul = split(jnp.concatenate([lg[0, nb, j], lg[1, nb, j]], axis=1))
-                prod = dot3(ch[nb, m], cl[nb, m], uh, ul)
-                real = prod[:ranks, :rank2] - prod[ranks:, rank2:]
-                imag = prod[:ranks, rank2:] + prod[ranks:, :rank2]
-                return real, imag
-
-            real, imag = product(0)
-
-            @pl.when(c > 0)
-            def _():
-                ks[j, m, 0] = real
-                ks[j, m, 1] = imag
-
-            @pl.when(c == 0)
-            def _():
-                real1, imag1 = product(1)
-                ks[j, m, 0] = real + real1
-                ks[j, m, 1] = imag + imag1
-
-            @pl.when(j != c)
+            @pl.when(m == 0)
+            def _():
+                for p in range(2):
+                    uh, ul = split(lg[p, j])
+                    lc[j, 0, :, p * rank2:(p + 1) * rank2] = uh
+                    lc[j, 1, :, p * rank2:(p + 1) * rank2] = ul
+
+            prod = stacked(cs[...], lc[j, 0], lc[j, 1])
+            ks[j, m, 0] = prod[:ranks, :rank2] - prod[ranks:, rank2:]
+            ks[j, m, 1] = prod[:ranks, rank2:] + prod[ranks:, :rank2]
+
+            @pl.when(jnp.logical_and(c == 1, j > 0))
+            def _():
+                k_next(j, m).wait_recv()
+                ks[j, m] = ks[j, m] + ku[j, m]
+
+            @pl.when(jnp.logical_and(c == 0, j > 0))
+            def _():
+                k_next(j, m).start()
+
+            @pl.when(jnp.logical_and(c > 0, j != c))
             def _():
                 k_out(j, m).start()
 
@@ -727,21 +799,22 @@
     half = width * tiles
     total = 2 * half
     final0 = jnp.where(c == 0, half + nsub - 1, (nsub - 1) * half + n_cols - 1 - c)
+    final0 = jnp.where(c == 1, total, final0)
 
     def unit(u, carry):
         i = u // half * width + u % width
         m = u // width % tiles
         t, s = ts(i)
 
-        @pl.when(active(i))
+        @pl.when(jnp.logical_and(active(i), u < total))
         def _():
             @pl.when(jnp.logical_and(c < 2, jnp.logical_and(u < half, u % width == 0)))
             def _():
-                x_swap(m).wait_recv()
                 for p in range(2):
+                    x_swap(m, p).wait_recv()
                     a, b = split(x0[m, p])
-                    xh[0, m, p * ranks:(p + 1) * ranks, :] = a
-                    xl[0, m, p * ranks:(p + 1) * ranks, :] = b
+                    xs[0, m, p * ranks:(p + 1) * ranks, :] = a
+                    xs[0, m, (p + 2) * ranks:(p + 3) * ranks, :] = b
 
             for e in range(2):
                 b = 2 * t + (h + e) % 2
@@ -756,8 +829,14 @@
                             side(t, s, 0, b).wait_recv()
 
                 def product(kk):
-                    uh, ul = split(jnp.concatenate([us[b, s, kk, 0], us[b, s, kk, 1]], axis=1))
-                    prod = dot3(xh[kk, m], xl[kk, m], uh, ul)
+                    @pl.when(m == 0)
+                    def _():
+                        for p in range(2):
+                            uh, ul = split(us[b, s, kk, p])
+                            uc[i, e, kk, 0, :, p * sw:(p + 1) * sw] = uh
+                            uc[i, e, kk, 1, :, p * sw:(p + 1) * sw] = ul
+
+                    prod = stacked(xs[kk, m], uc[i, e, kk, 0], uc[i, e, kk, 1])
                     real = prod[:ranks, :sw] - prod[ranks:, sw:]
                     imag = prod[:ranks, sw:] + prod[ranks:, :sw]
                     return real, imag
@@ -789,11 +868,24 @@
         def _():
             finish_next(m)
 
-        @pl.when(jnp.logical_and(c != 1, jnp.logical_or(u == final0, u == final0 + width)))
+        @pl.when(jnp.logical_or(u == final0, u == final0 + width))
         def _():
             finish(m)
 
-        @pl.when(jnp.logical_and(c < 2, u == width - 1))
+        @pl.when(jnp.logical_and(c == 0, u < width))
+        def _():
+            relay_native(width + u)
+
+        @pl.when(u == jnp.where(c == 0, half - 1, jnp.where(c == 1, total - 1, width - 1)))
+        def _():
+            gather()
+
+        @pl.when(jnp.logical_and(c == 1, u == 0))
+        def _():
+            for i in range(width, stages):
+                lift_in(i)
+
+        @pl.when(jnp.logical_and(c == 1, u == width - 1))
         def _():
             for i in range(width, stages):
                 relay_native(i)
@@ -803,56 +895,44 @@
         def _():
             for i in range(width, stages):
                 collect(i)
-
-            @pl.when(c == 0)
-            def _():
-                others(spread)
+            each(0, jnp.where(c == 1, 1, 0), spread)
 
         return carry
 
-    lax.fori_loop(0, total, unit, 0)
-
-    @pl.when(c == 1)
-    def _():
-        entries_in()
-        for m in range(tiles):
-            q_up(m).wait_recv()
-            panel_ref[m] = pin[m]
+    lax.fori_loop(0, jnp.where(c == 1, total + 2 * width - 1, total), unit, 0)
 
     for m in range(tiles):
-        @pl.when(c != 1)
-        def _():
-            cores_ref[m, 0] = ks[c, m]
-
-        @pl.when(c == 1)
-        def _():
-            cores_ref[m, 0] = jnp.zeros_like(ks[c, m])
+        cores_ref[m, 0] = ks[c, m]
 
         def add(o):
-            @pl.when(o != 1)
+            @pl.when(o > 0)
             def _():
                 rcopy(ks.at[c, m], kd.at[o, m], k_send.at[c, m], k_recv.at[o, m], sib).wait_recv()
                 cores_ref[m, 0] = cores_ref[m, 0] + kd[o, m]
 
         others(add)
-
-    @pl.when(sender)
-    def _():
-        for s in range(nsub):
-            each(0, chips, lambda g: lift_out(s, g).wait_send())
 
     @pl.when(c < 2)
     def _():
         for m in range(tiles):
-            @pl.when(jnp.logical_or(c == 1, m > 0))
-            def _():
-                x_swap(m).wait_send()
+            for p in range(2):
+                x_swap(m, p).wait_send()
+        for s in range(nsub):
+            for t in range(1, n_cols):
+                @pl.when(c == (0 if t > 1 else 1))
+                def _():
+                    raised(t, s, stg.at[t % width, s]).wait_send()
 
     @pl.when(c == 0)
     def _():
         for m in range(tiles):
             q_up(m).wait_send()
 
+    @pl.when(source)
+    def _():
+        for s in range(nsub):
+            each(1, chips, lambda d: scatter(s, ahead(d)).wait_send())
+
     def drain(i):
         t, s = ts(i)
 
@@ -866,8 +946,11 @@
 
             @pl.when(yn == t)
             def _():
-                for k in range(2):
-                    nat_half(t, s, k, half1).wait_send()
+                nat_half(t, s, 1, half1).wait_send()
+
+            @pl.when(jnp.where(c == 0, xn == t, yn == t))
+            def _():
+                nat_half(t, s, 0, half1).wait_send()
 
             side(t, s, 1, 2 * t + h).wait_send()
 
@@ -888,19 +971,18 @@
     each(0, stages, drain)
 
     def tail_l(j):
-        def left(nb):
-            each(1, chips, lambda d: g_out(j, nb, d).wait_send())
-            l_sib(j, nb, h).wait_send()
-
-        blocks(c, left)
-        blocks(j, lambda nb: l_out(j, nb).wait_send())
-
-        @pl.when(c != 1)
-        def _():
-            for m in range(tiles):
-                k_out(j, m).wait_send()
-
-    others(tail_l)
+        each(1, chips, lambda d: g_out(j, d).wait_send())
+        l_down(j).wait_send()
+
+    each(0, c, tail_l)
+    each(c + 1, n_cols, lambda o: l_up(o).wait_send())
+
+    def tail_k(j):
+        l_sib(j, h).wait_send()
+        for m in range(tiles):
+            k_out(j, m).wait_send()
+
+    others(tail_k)
     each(1, n_cols, lambda k: e_out(k).wait_send())
 
 
@@ -925,32 +1007,35 @@
         in_specs=[vmem, hbm, hbm, vmem, vmem, pl.BlockSpec(memory_space=pltpu.SMEM)],
         out_specs=(vmem, vmem),
         scratch_shapes=[
-            pltpu.VMEM((2, tiles, 2 * ranks, wc), bf16),
-            pltpu.VMEM((2, tiles, 2 * ranks, wc), bf16),
+            pltpu.VMEM((2, tiles, 4 * ranks, wc), bf16),
             pltpu.VMEM((tiles, 2, ranks, wc), f32),
-            pltpu.VMEM((2, tiles, 2 * ranks, wc), bf16),
-            pltpu.VMEM((2, tiles, 2 * ranks, wc), bf16),
+            pltpu.VMEM((4 * ranks, wc), bf16),
             pltpu.VMEM((n_rows, nsub, 2, 2, wc, sw), f32),
+            pltpu.VMEM((2 * nsub, 2, 2, 2, wc, 2 * sw), bf16),
+            pltpu.VMEM((n_cols, 2, wc, 2 * left_ranks), bf16),
+            pltpu.VMEM((n_cols - 2, nsub, 2, wc // chips, sw), f32),
             sums,
             sums,
             pltpu.VMEM((tiles, 2, ranks, wc), f32),
             pltpu.VMEM((tiles, 2, ranks, wc), f32),
-            pltpu.VMEM((2, 2, n_cols, wc, left_ranks), f32),
+            pltpu.VMEM((2, n_cols, wc, left_ranks), f32),
+            pltpu.VMEM((n_cols, tiles, 2, ranks, left_ranks), f32),
             pltpu.VMEM((n_cols, tiles, 2, ranks, left_ranks), f32),
             pltpu.VMEM((n_cols, tiles, 2, ranks, left_ranks), f32),
             pltpu.VMEM((n_cols, -(-2 * tiles // 8) * 8, ranks), f32),
             dma((nsub,)), dma((nsub,)), dma((nsub, 2)), dma((n_cols, nsub, 2)), dma((n_cols, nsub)),
             dma((n_cols, nsub, 2)), dma((n_cols, nsub, 2)),
-            dma((nsub, chips)), dma((n_cols, nsub, chips)), dma((n_cols, nsub, 2)),
+            dma((nsub, n_cols)), dma((nsub, chips)), dma((n_cols - 2, nsub)),
+            dma((n_cols, nsub, chips)), dma((n_cols, nsub, 2)),
             dma((n_cols, nsub)), dma((n_cols, nsub)), dma((n_cols, nsub)), dma((n_cols, nsub)),
-            dma((n_cols, nsub, 2)), dma((n_cols, nsub, 2)), dma((tiles,)), dma((tiles,)),
+            dma((n_cols, nsub, 2)), dma((n_cols, nsub, 2)), dma((tiles, 2)), dma((tiles, 2)),
             dma((n_rows, nsub, tiles)), dma((n_rows, nsub, tiles)), dma((tiles,)), dma((tiles,)),
-            dma((2,)), dma((n_cols, 2)), dma((n_cols, 2)), dma((n_cols, 2, chips)), dma((n_cols, 2, chips)),
-            dma((n_cols, 2)), dma((n_cols, 2)),
-            dma((n_cols, tiles)), dma((n_cols, tiles)), dma((n_cols,)), dma((n_cols,)),
+            dma((1,)), dma((n_cols,)), dma((n_cols,)), dma((n_cols, chips)), dma((n_cols, chips)),
+            dma((n_cols,)), dma((n_cols,)),
+            dma((n_cols, tiles)), dma((n_cols, tiles)), dma((n_cols, tiles)), dma((n_cols,)), dma((n_cols,)),
         ],
         compiler_params=pltpu.CompilerParams(
-            collective_id=0, has_side_effects=True, vmem_limit_bytes=56 * 1024 * 1024
+            collective_id=0, has_side_effects=True, vmem_limit_bytes=60 * 1024 * 1024
         ),
     )(row_samples, upper_inverse, upanel_left, col_samples, pivot_rows, rank_blocks)
 

time: 140 us -> 111 us (0.79); the launches traced: 138 us -> 110 us
  Pallas kernels: 134 us -> 107 us
    pallas_call x1, Pallas kernels: 134 us -> 107 us  [paired(): pl.pallas_call(functools.partial(paired_kernel, n_rows, n_cols), out_shap...]
where the time goes in v3:
time: 111 us; the launch traced here: 110 us
  Pallas kernels  107 us (96%)
  local copies, waits for them, and re-layouts  3.01 us (3%)
    pallas_call x1, Pallas kernels, paired(): pl.pallas_call(functools.partial(paired_kernel, n_rows, n_cols), out_shap...  107 us
    unnamed x4, local copies, waits for them, and re-layouts  3.01 us

profile of v3, /device:TPU:28, one launch (start us, length us, event | category | flops | bytes accessed | tf_op | source)
XLA Modules:
  0.0 110.3 jit_solution(1320293669923092908)
XLA Ops:
  0.6 106.7 %shard_map.77 = (f32[2,2,128,512]{3,2,1,0:T(8,128)}, f32[2,1,2,128,128]{4,3,2,1,0:T(8,128)}) custom-call(f32[2,2,128,512]{3,2,1,0:T(8,128)} %row_ref.1, f32[2,512,256]{2,1,0:T(8,128)} %u_ref.1, f32[1,2,2048,128]{3,2,1,0:T(8,128)} %up_ref.1, f32[2,2,512,128]{3,2,1,0:T(8,128)} %col_ref.1, s32[2,128]{1,0:T(2,128)} %piv_ref.1, s32[2]{0:T(128)} %rank_ref.1), custom_call_target="tpu_custom_call" | custom-call | tf_op jit(solution)/shard_map/pallas_call | solution.py:1001
  107.3 0.0 copy-start
  107.3 2.3 %copy.10 = f32[2,2,128,512]{3,2,1,0:T(8,128)} copy(f32[2,2,128,512]{3,2,1,0:T(8,128)} %get-tuple-element.4) | data formatting | bytes 2097152
  109.6 0.0 copy-done
  109.6 0.7 copy.11
Async XLA Ops:
  107.3 2.3 %copy-start = (f32[2,1,2,128,128]{4,3,2,1,0:T(8,128)S(1)}, f32[2,1,2,128,128]{4,3,2,1,0:T(8,128)}, u32[]{:S(2)}) copy-start(f32[2,1,2,128,128]{4,3,2,1,0:T(8,128)} %get-tuple-element.5) | copy-start | bytes 786436

commit v4 on v3

--- a/solution.py
+++ b/solution.py
@@ -341,7 +341,7 @@
     n_rows, n_cols,
     row_ref, u_ref, up_ref, col_ref, piv_ref, rank_ref,
     panel_ref, cores_ref,
-    xs, x0, cs, us, uc, lc, stg, ps, pr, pq, pin, lg, ks, ku, kd, eb,
+    rows, cols, in_sem, xs, x0, cs, us, uc, lc, stg, ps, pr, pq, pin, lg, ks, ku, kd, eb,
     u_loc, nat_x, nat_y, nat_fwd, full1, near1, half1,
     lift, sc_send, sc_recv, full0, half0, lift_x, lift_y, lift_fx, lift_fy,
     side_send, side_recv, x_send, x_recv, p_send, p_recv, q_send, q_recv,
@@ -469,11 +469,24 @@
         return rcopy(ks.at[j, m], kd.at[c, m], k_send.at[j, m], k_recv.at[c, m], (r, j))
 
     def k_next(j, m):
-        return rcopy(ks.at[j, m], ku.at[j, m], k_send.at[j, m], ku_recv.at[j, m], (r, 1))
+        to = (r, jnp.where(c == 0, 1, n_cols - 2))
+        return rcopy(ks.at[j, m], ku.at[j, m], k_send.at[j, m], ku_recv.at[j, m], to)
+
+    def join(j, m):
+        k_next(j, m).wait_recv()
+        ks[j, m] = ks[j, m] + ku[j, m]
+
+        @pl.when(j != c)
+        def _():
+            k_out(j, m).start()
 
     def e_out(k):
         return rcopy(eb.at[c], eb.at[c], e_send.at[k], e_recv.at[c], (r, (c + k) % n_cols))
 
+    row_in = pltpu.make_async_copy(row_ref, rows, in_sem.at[0])
+    col_in = pltpu.make_async_copy(col_ref, cols, in_sem.at[1])
+    col_in.start()
+    row_in.start()
     l_own().start()
     barrier = pltpu.get_barrier_semaphore()
 
@@ -519,6 +532,18 @@
             lift_full(t, s, q, lift_x, to_x).start()
             lift_full(t, s, q, lift_y, to_y).start()
 
+    def relay_x(i):
+        t, s = ts(i)
+
+        @pl.when(jnp.logical_and(c == 0, xn == t))
+        def _():
+            nat_full(t, s).wait_recv()
+            nat_half(t, s, 0, half1, to_y).start()
+
+            @pl.when(t == 0)
+            def _():
+                nat_half(t, s, 1, half1, to_y).start()
+
     def relay_native(i):
         t, s = ts(i)
 
@@ -531,12 +556,14 @@
                 nat_half(t, s, 0, half1).start()
 
             nat_half(t, s, 1, near1).wait_recv()
-            nat_half(t, s, 1, half1).start()
-
-        @pl.when(jnp.logical_and(c == 0, xn == t))
-        def _():
-            nat_full(t, s).wait_recv()
-            nat_half(t, s, 0, half1, to_y).start()
+
+            @pl.when(jnp.logical_or(c > 0, t > 0))
+            def _():
+                nat_half(t, s, 1, half1).start()
+
+        @pl.when(jnp.asarray(i) < width)
+        def _():
+            relay_x(i)
 
     def relay_lift(i):
         t, s = ts(i)
@@ -585,6 +612,7 @@
         scatters(s)
 
     each(0, stages, lambda i: pl.when(jnp.logical_or(c > 1, i < width))(lambda: native_out(i)))
+
     def climb(t, s):
         @pl.when(q == t)
         def _():
@@ -617,12 +645,13 @@
     def _():
         l_down(0).start()
 
+    col_in.wait()
     pos = c * wc + lax.broadcasted_iota(jnp.int32, (wc, ranks), 0)
     parts = []
     for i in range(tiles):
         hit = pos == piv_ref[i:i + 1, :]
         for p in range(2):
-            parts.append(jnp.sum(jnp.where(hit, col_ref[i, p], 0.0), axis=0, keepdims=True))
+            parts.append(jnp.sum(jnp.where(hit, cols[i, p], 0.0), axis=0, keepdims=True))
     parts.append(jnp.zeros((eb.shape[1] - 2 * tiles, ranks), jnp.float32))
     eb[c] = jnp.concatenate(parts, axis=0)
     each(1, n_cols, lambda k: e_out(k).start())
@@ -648,12 +677,13 @@
 
         @pl.when(c == 0)
         def _():
-            native_y(width)
             relay_lift(0)
             relay_lift(1)
             relay_native(1)
-            for i in range(width + 1, stages):
+            for i in range(width, stages):
                 native_y(i)
+            for i in range(width, stages):
+                relay_x(i)
 
         @pl.when(c == 1)
         def _():
@@ -674,9 +704,10 @@
         each(0, c, spread)
 
 
+    row_in.wait()
     for m in range(tiles):
         for p in range(2):
-            a, b = split(row_ref[m, p])
+            a, b = split(rows[m, p])
             xs[1, m, p * ranks:(p + 1) * ranks, :] = a
             xs[1, m, (p + 2) * ranks:(p + 3) * ranks, :] = b
 
@@ -781,14 +812,15 @@
 
             @pl.when(jnp.logical_and(c == 1, j > 0))
             def _():
-                k_next(j, m).wait_recv()
-                ks[j, m] = ks[j, m] + ku[j, m]
-
-            @pl.when(jnp.logical_and(c == 0, j > 0))
+                join(j, m)
+
+            ends = jnp.logical_or(c == 0, c == n_cols - 1)
+
+            @pl.when(jnp.logical_and(ends, j != c))
             def _():
                 k_next(j, m).start()
 
-            @pl.when(jnp.logical_and(c > 0, j != c))
+            @pl.when(jnp.logical_or(jnp.logical_and(c == 1, j == 0), jnp.logical_and(c == n_cols - 2, j > c)))
             def _():
                 k_out(j, m).start()
 
@@ -872,11 +904,15 @@
         def _():
             finish(m)
 
-        @pl.when(jnp.logical_and(c == 0, u < width))
-        def _():
-            relay_native(width + u)
-
-        @pl.when(u == jnp.where(c == 0, half - 1, jnp.where(c == 1, total - 1, width - 1)))
+        @pl.when(jnp.logical_and(c == 0, jnp.logical_and(u >= width, u < half)))
+        def _():
+            relay_native(u)
+
+        @pl.when(jnp.logical_and(c == n_cols - 2, u >= total - 2))
+        def _():
+            each(0, c + 1, lambda j: join(j, u - total + 2))
+
+        @pl.when(u == jnp.where(c == 0, half, jnp.where(c == 1, total - 1, width - 1)))
         def _():
             gather()
 
@@ -900,17 +936,6 @@
         return carry
 
     lax.fori_loop(0, jnp.where(c == 1, total + 2 * width - 1, total), unit, 0)
-
-    for m in range(tiles):
-        cores_ref[m, 0] = ks[c, m]
-
-        def add(o):
-            @pl.when(o > 0)
-            def _():
-                rcopy(ks.at[c, m], kd.at[o, m], k_send.at[c, m], k_recv.at[o, m], sib).wait_recv()
-                cores_ref[m, 0] = cores_ref[m, 0] + kd[o, m]
-
-        others(add)
 
     @pl.when(c < 2)
     def _():
@@ -944,7 +969,7 @@
                 for k in range(2):
                     nat_near(s, k).wait_send()
 
-            @pl.when(yn == t)
+            @pl.when(jnp.where(jnp.logical_and(c == 0, t == 0), xn == t, yn == t))
             def _():
                 nat_half(t, s, 1, half1).wait_send()
 
@@ -984,6 +1009,17 @@
 
     others(tail_k)
     each(1, n_cols, lambda k: e_out(k).wait_send())
+
+    for m in range(tiles):
+        cores_ref[m, 0] = ks[c, m]
+
+        def add(o):
+            @pl.when(jnp.logical_and(o > 0, o < n_cols - 1))
+            def _():
+                rcopy(ks.at[c, m], kd.at[o, m], k_send.at[c, m], k_recv.at[o, m], sib).wait_recv()
+                cores_ref[m, 0] = cores_ref[m, 0] + kd[o, m]
+
+        others(add)
 
 
 def paired(n_rows, n_cols, col_samples, row_samples, pivot_rows, rank_blocks, upper_inverse, upanel_left):
@@ -1004,9 +1040,12 @@
             jax.ShapeDtypeStruct((tiles, 2, ranks, wc), f32),
             jax.ShapeDtypeStruct((tiles, 1, 2, ranks, left_ranks), f32),
         ),
-        in_specs=[vmem, hbm, hbm, vmem, vmem, pl.BlockSpec(memory_space=pltpu.SMEM)],
+        in_specs=[hbm, hbm, hbm, hbm, vmem, pl.BlockSpec(memory_space=pltpu.SMEM)],
         out_specs=(vmem, vmem),
         scratch_shapes=[
+            pltpu.VMEM(row_samples.shape, f32),
+            pltpu.VMEM(col_samples.shape, f32),
+            dma((2,)),
             pltpu.VMEM((2, tiles, 4 * ranks, wc), bf16),
             pltpu.VMEM((tiles, 2, ranks, wc), f32),
             pltpu.VMEM((4 * ranks, wc), bf16),

time: 111 us -> 108 us (0.973)
  Pallas kernels: 107 us -> 103 us
    pallas_call x1, Pallas kernels: 107 us -> 103 us  [paired(): pl.pallas_call(functools.partial(paired_kernel, n_rows, n_cols), out_shap...]
where the time goes in v4:
time: 108 us; the launch traced here: 106 us
  Pallas kernels  103 us (95%)
  local copies, waits for them, and re-layouts  3.01 us (3%)
    pallas_call x1, Pallas kernels, paired(): pl.pallas_call(functools.partial(paired_kernel, n_rows, n_cols), out_shap...  103 us
    unnamed x4, local copies, waits for them, and re-layouts  3.01 us

profile of v4, /device:TPU:28, one launch (start us, length us, event | category | flops | bytes accessed | tf_op | source)
XLA Modules:
  0.0 106.3 jit_solution(14823160384153221051)
XLA Ops:
  0.6 102.6 %shard_map.77 = (f32[2,2,128,512]{3,2,1,0:T(8,128)}, f32[2,1,2,128,128]{4,3,2,1,0:T(8,128)}) custom-call(f32[2,2,128,512]{3,2,1,0:T(8,128)} %row_ref.1, f32[2,512,256]{2,1,0:T(8,128)} %u_ref.1, f32[1,2,2048,128]{3,2,1,0:T(8,128)} %up_ref.1, f32[2,2,512,128]{3,2,1,0:T(8,128)} %col_ref.1, s32[2,128]{1,0:T(2,128)} %piv_ref.1, s32[2]{0:T(128)} %rank_ref.1), custom_call_target="tpu_custom_call" | custom-call | tf_op jit(solution)/shard_map/pallas_call | solution.py:1037
  103.3 0.0 copy-start
  103.3 2.3 %copy.10 = f32[2,2,128,512]{3,2,1,0:T(8,128)} copy(f32[2,2,128,512]{3,2,1,0:T(8,128)} %get-tuple-element.4) | data formatting | bytes 2097152
  105.6 0.0 copy-done
  105.6 0.7 copy.11
Async XLA Ops:
  103.3 2.3 %copy-start = (f32[2,1,2,128,128]{4,3,2,1,0:T(8,128)S(1)}, f32[2,1,2,128,128]{4,3,2,1,0:T(8,128)}, u32[]{:S(2)}) copy-start(f32[2,1,2,128,128]{4,3,2,1,0:T(8,128)} %get-tuple-element.5) | copy-start | bytes 786436

commit v5 on v4

--- a/solution.py
+++ b/solution.py
@@ -693,8 +693,12 @@
             for i in range(width, stages):
                 native_out(i)
 
-        for i in range(width):
-            collect(i)
+        collect(0)
+
+        @pl.when(c == 0)
+        def _():
+            for i in range(1, width):
+                collect(i)
 
     @pl.when(c > 1)
     def _():
@@ -798,7 +802,8 @@
             cs[p * ranks:(p + 1) * ranks, :] = a
             cs[(p + 2) * ranks:(p + 3) * ranks, :] = b
 
-        def core(j, carry):
+        def core(index, carry):
+            j = jnp.where(c == n_cols - 1, index, (n_cols - index) % n_cols)
             @pl.when(m == 0)
             def _():
                 for p in range(2):
@@ -912,6 +917,12 @@
         def _():
             each(0, c + 1, lambda j: join(j, u - total + 2))
 
+        @pl.when(jnp.logical_and(c == 1, jnp.logical_or(u == 0, u == half)))
+        def _():
+            base = u // half * width
+            for k in range(1, width):
+                collect(base + k)
+
         @pl.when(u == jnp.where(c == 0, half, jnp.where(c == 1, total - 1, width - 1)))
         def _():
             gather()
@@ -929,8 +940,13 @@
 
         @pl.when(jnp.logical_and(c < 2, u == half - 1))
         def _():
-            for i in range(width, stages):
-                collect(i)
+            collect(width)
+
+            @pl.when(c == 0)
+            def _():
+                for i in range(width + 1, stages):
+                    collect(i)
+
             each(0, jnp.where(c == 1, 1, 0), spread)
 
         return carry

time: 108 us -> 107 us (level)
  the two profiles are of different devices: /device:TPU:28 before, /device:TPU:0 now
where the time goes in v5:
time: 107 us
  Pallas kernels  103 us (96%)
  local copies, waits for them, and re-layouts  3.01 us (3%)
    pallas_call x1, Pallas kernels, paired(): pl.pallas_call(functools.partial(paired_kernel, n_rows, n_cols), out_shap...  103 us
    unnamed x4, local copies, waits for them, and re-layouts  3.01 us

profile of v5, /device:TPU:0, one launch (start us, length us, event | category | flops | bytes accessed | tf_op | source)
XLA Modules:
  0.0 107.0 jit_solution(14208526697413133208)
XLA Ops:
  0.6 103.3 %shard_map.77 = (f32[2,2,128,512]{3,2,1,0:T(8,128)}, f32[2,1,2,128,128]{4,3,2,1,0:T(8,128)}) custom-call(f32[2,2,128,512]{3,2,1,0:T(8,128)} %row_ref.1, f32[2,512,256]{2,1,0:T(8,128)} %u_ref.1, f32[1,2,2048,128]{3,2,1,0:T(8,128)} %up_ref.1, f32[2,2,512,128]{3,2,1,0:T(8,128)} %col_ref.1, s32[2,128]{1,0:T(2,128)} %piv_ref.1, s32[2]{0:T(128)} %rank_ref.1), custom_call_target="tpu_custom_call" | custom-call | tf_op jit(solution)/shard_map/pallas_call | solution.py:1053
  104.0 0.0 copy-start
  104.0 2.3 %copy.10 = f32[2,2,128,512]{3,2,1,0:T(8,128)} copy(f32[2,2,128,512]{3,2,1,0:T(8,128)} %get-tuple-element.4) | data formatting | bytes 2097152
  106.3 0.0 copy-done
  106.3 0.7 copy.11
Async XLA Ops:
  104.0 2.3 %copy-start = (f32[2,1,2,128,128]{4,3,2,1,0:T(8,128)S(1)}, f32[2,1,2,128,128]{4,3,2,1,0:T(8,128)}, u32[]{:S(2)}) copy-start(f32[2,1,2,128,128]{4,3,2,1,0:T(8,128)} %get-tuple-element.5) | copy-start | bytes 786436
